TPU v7x, 1024 devices: a whole 8x8x8 slice. The times are simulated.
1024 devices in a mesh: dom: 512 (over x, z, y), orb: 2 (over core).
Axes of the slice: x: 8, y: 8, z: 8, core: 2. Of those that a mesh axis runs over, the one named last changes fastest.
Arguments:
- block: float32 [256, 346112], P('orb', 'dom')
- conn: int32 [125, 4608], P(None, 'dom'), may hold values from 0 to 844, as said below
- bottom: int32 [86528], P('dom'), may hold values from 0 to 675, as said below
- cell_scale: float32 [4608], P('dom'), may hold values from 0.5 to 2
- potential: float32 [216, 4608], P(None, 'dom'), may hold values from 0.1 to 1
- mass: float32 [346112], P('dom'), may hold values from 0.5 to 2
- stiffness: float32 [125, 125], replicated, as said below
- interp: float32 [216, 125], replicated, may hold values from -0.5 to 0.5
- occupancy: float32 [256], P('orb'), may hold values from 0.2 to 2
- spectrum: float32 [2], replicated, as said below
Outputs:
- density: float32 [216, 4608], P(None, 'dom')
Inputs may be any that keep to these rules, and one draw needn't show every extreme that they name: `conn`: for the cells of domain d an entry below 676 is one of d's own local node numbers and 676 + f names entry f of the next domain's list in bottom; every own node is named by some cell of its domain, and the cells form a conforming mesh. `bottom`: each domain's 169 entries are distinct local numbers of its own nodes. `stiffness`: symmetric and positive definite. spectrum[0] < spectrum[1].
All inputs are finite; a program needn't handle non-finite values.
Results may differ from a plain program's by a relative error of at most 0.0001.
Values sent between devices are 32-bit elements; how exact they have to be, the bound alone decides.
No kernel may reach another device: no remote copies, remote signals or barrier semaphores. Data moves between devices by JAX's collectives and lax.ppermute only.
A program may use at most 32 MiB of HBM per device.

v0:
```python
import jax
import jax.numpy as jnp
from jax import lax
from jax.sharding import PartitionSpec as P

ORBS = 256
DEG = 3


def shifted(value, axis, steps):
    count = lax.axis_size(axis)
    initial, last = (max(0, -steps), min(count, count - steps))
    return lax.ppermute(value, axis, [(source, source + steps) for source in range(initial, last)])


def cell_values(ext, conn):
    orbs = ext.shape[0]
    npc, cells = conn.shape
    picked = jnp.take(ext, conn.reshape(-1), axis=1).reshape(orbs, npc, cells)
    return jnp.transpose(picked, (1, 0, 2)).reshape(npc, orbs * cells)


def cell_apply(ext, conn, cell_scale, potential, stiffness, interp):
    orbs = ext.shape[0]
    npc, cells = conn.shape
    local = cell_values(ext, conn)
    stiff = jnp.dot(
        stiffness, local, precision=lax.Precision.HIGHEST, preferred_element_type=jnp.float32
    )
    quad = jnp.dot(
        interp, local, precision=lax.Precision.HIGHEST, preferred_element_type=jnp.float32
    )
    quad = quad.reshape(-1, orbs, cells) * potential[:, None, :]
    back = jnp.dot(
        interp.T,
        quad.reshape(-1, orbs * cells),
        precision=lax.Precision.HIGHEST,
        preferred_element_type=jnp.float32,
    )
    total = stiff.reshape(npc, orbs, cells) * cell_scale[None, None, :] + back.reshape(
        npc, orbs, cells
    )
    values = jnp.transpose(total, (1, 0, 2)).reshape(orbs, npc * cells)
    return jnp.zeros_like(ext).at[:, conn.reshape(-1)].add(values)


def density_terms(ext, conn, interp, occupancy):
    orbs = ext.shape[0]
    npc, cells = conn.shape
    local = cell_values(ext, conn)
    quad = jnp.dot(
        interp, local, precision=lax.Precision.HIGHEST, preferred_element_type=jnp.float32
    )
    quad = quad.reshape(-1, orbs, cells)
    return jnp.sum(occupancy[None, :, None] * quad * quad, axis=1) / ORBS


def fetch_face(field, bottom):
    return shifted(field[:, bottom], "dom", -1)


def apply_operator(field, conn, bottom, cell_scale, potential, mass, stiffness, interp):
    node_dev = field.shape[1]
    ext = jnp.concatenate([field, fetch_face(field, bottom)], axis=1)
    partial_value = cell_apply(ext, conn, cell_scale, potential, stiffness, interp)
    incoming = shifted(partial_value[:, node_dev:], "dom", 1)
    return partial_value[:, :node_dev].at[:, bottom].add(incoming) / mass[None, :]


def per_device(
    block, conn, bottom, cell_scale, potential, mass, stiffness, interp, occupancy, spectrum
):
    own_orbs = block.shape[0]
    node_dev = block.shape[1]
    total_orbs = own_orbs * lax.axis_size("orb")
    total_nodes = node_dev * lax.axis_size("dom")
    halfwidth = (spectrum[1] - spectrum[0]) / 2.0
    centre = (spectrum[1] + spectrum[0]) / 2.0

    def operator(values):
        return apply_operator(values, conn, bottom, cell_scale, potential, mass, stiffness, interp)

    previous = block
    current = (operator(block) - centre * block) / halfwidth
    for step in range(DEG - 1):
        following = 2.0 * (operator(current) - centre * current) / halfwidth - previous
        previous = current
        current = following
    identity = jnp.eye(total_orbs, dtype=jnp.float32)
    ext = jnp.concatenate([current, fetch_face(current, bottom)], axis=1)
    whole = lax.all_gather(ext, "orb", axis=0, tiled=True)
    owned = whole[:, :node_dev]
    term = jnp.dot(
        owned * mass[None, :],
        owned.T,
        precision=lax.Precision.HIGHEST,
        preferred_element_type=jnp.float32,
    )
    gram = lax.psum(term, "dom") / total_nodes
    multiplier = jnp.linalg.cholesky(gram)
    inverse = jax.scipy.linalg.solve_triangular(multiplier, identity, lower=True)
    rows = lax.dynamic_slice_in_dim(inverse, lax.axis_index("orb") * own_orbs, own_orbs, 0)
    ortho_ext = jnp.dot(
        rows, whole, precision=lax.Precision.HIGHEST, preferred_element_type=jnp.float32
    )
    terms = density_terms(ortho_ext, conn, interp, occupancy)
    return lax.psum(terms, "orb")


def solution(mesh):
    in_specs = (
        P("orb", "dom"),
        P(None, "dom"),
        P("dom"),
        P("dom"),
        P(None, "dom"),
        P("dom"),
        P(),
        P(),
        P("orb"),
        P(),
    )
    out_specs = P(None, "dom")
    return jax.shard_map(
        per_device, mesh=mesh, in_specs=in_specs, out_specs=out_specs, check_vma=False
    )
```

profile of v0, /device:TPU:1, one launch (start us, length us, event | category | flops | bytes accessed | tf_op | source)
XLA Modules:
  0.0 503.3 jit_solution(14756503504979466325)
XLA Ops:
  15.0 2.4 gather_fusion.4
  28.5 2.4 add_bitcast_fusion.2
  32.9 8.2 %scatter_custom_fusion = f32[128,845]{0,1:T(8,128)S(1)} fusion(s32[1125]{0:T(1024)S(1)} %fusion.34, f32[128,1125]{0,1:T(8,128)S(1)} %reshape.240, f32[]{:T(128)} %constant.106.clone.1), kind=kCustom, calls=%fused_computation.43 | custom fusion | flops 144000 | bytes 1010180 | tf_op jit(solution)/shard_map/scatter-add | solution.py:44
  41.2 4.0 collective-permute-start.1
  52.5 3.8 collective-permute-done.2
  56.3 2.4 gather_fusion.5
  71.6 2.4 add_bitcast_fusion.1
  76.9 8.5 %scatter_custom_fusion.2 = f32[128,845]{0,1:T(8,128)S(1)} fusion(s32[1125]{0:T(1024)S(1)} %fusion.34, f32[128,1125]{0,1:T(8,128)} %reshape.256, f32[]{:T(128)} %constant.106.clone.1), kind=kCustom, calls=%fused_computation.41 | custom fusion | flops 144000 | bytes 1008644 | tf_op jit(solution)/shard_map/scatter-add | solution.py:44
  85.4 3.9 collective-permute-start.3
  94.7 4.4 collective-permute-done.4
  99.2 2.4 gather_fusion.6
  114.7 8.2 %scatter_custom_fusion.4 = f32[128,845]{0,1:T(8,128)S(1)} fusion(s32[1125]{0:T(1024)S(1)} %fusion.34, f32[128,1125]{0,1:T(8,128)S(1)} %reshape.272, f32[]{:T(128)} %constant.106.clone.1), kind=kCustom, calls=%fused_computation.39 | custom fusion | flops 144000 | bytes 1010180 | tf_op jit(solution)/shard_map/scatter-add | solution.py:44
  123.0 4.6 collective-permute-start.5
  132.9 4.3 collective-permute-done.6
  137.2 19.2 %all_gather.3 = f32[256,845]{0,1:T(8,128)S(1)} all-gather(f32[128,845]{0,1:T(8,128)S(1)} %pad_maximum_fusion.3), channel_id=1, replica_groups=mesh['dom'=512,'orb'=2] {'orb'}, dimensions={0}, use_global_device_ids=true | all-gather | bytes 1297920 | tf_op jit(solution)/shard_map/all_gather | solution.py:91
  156.5 2.3 fusion.4
  158.9 259.9 %all-reduce.3.cloned.1.call-done = f32[256,256]{0,1:T(8,128)} async-done(((f32[256,256]{0,1:T(8,128)}), f32[256,256]{0,1:T(8,128)}) %all-reduce.3.cloned.1.call-update) | async-done | bytes 262160 | tf_op jit(solution)/shard_map/psum | solution.py:99
  420.0 11.7 %cholesky.50 = f32[128,128]{1,0:T(8,128)S(1)} custom-call(f32[128,128]{1,0:T(8,128)S(1)} %cholesky.118), custom_call_target="Cholesky" | custom-call | tf_op jit(solution)/shard_map/jit(cholesky)/cholesky | solution.py:100
  431.7 9.8 %custom-call.15 = f32[1,128,128]{1,2,0:T(8,128)S(1)} custom-call(f32[1,128,128]{2,1,0:T(8,128)S(1)} %get-tuple-element.27), custom_call_target="InvertDiagBlocksLowerTriangular" | custom-call | tf_op jit(solution)/shard_map/jit(cholesky)/cholesky | solution.py:100
  442.0 11.7 %cholesky.105 = f32[128,128]{1,0:T(8,128)S(1)} custom-call(f32[128,128]{1,0:T(8,128)S(1)} %convolution_subtract_fusion.1), custom_call_target="Cholesky" | custom-call | tf_op jit(solution)/shard_map/jit(cholesky)/cholesky | solution.py:100
  455.9 4.2 while.1
  460.1 19.7 %custom-call.16 = f32[2,128,128]{1,2,0:T(8,128)S(1)} custom-call(f32[2,128,128]{2,1,0:T(8,128)S(1)} %get-tuple-element.13), custom_call_target="InvertDiagBlocksLowerTriangular" | custom-call | tf_op jit(solution)/shard_map/jit(_solve_triangular)/triangular_solve | solution.py:101
  481.5 2.4 gather_fusion.7
  487.5 8.8 %psum.15 = f32[216,9]{0,1:T(8,128)} all-reduce(f32[216,9]{0,1:T(8,128)S(1)} %broadcast_multiply_fusion.1), channel_id=1, replica_groups=mesh['dom'=512,'orb'=2] {'orb'}, use_global_device_ids=true, to_apply=%region_12.14 | all-reduce | flops 1944 | bytes 15552 | tf_op jit(solution)/shard_map/psum | solution.py:107
  (130 shorter events, 77.4 us)
Async XLA Ops:
  6.5 14.1 %copy-start = (f32[216,125]{1,0:T(8,128)S(1)}, f32[216,125]{1,0:T(8,128)}, u32[]{:S(2)}) copy-start(f32[216,125]{1,0:T(8,128)} %param.19) | copy-start | bytes 324004
  6.5 3.7 copy-start.6
  6.5 4.2 copy-start.5
  6.5 412.2 %all-reduce.3.cloned.1.call-start = ((), (), s32[]{:S(2)}) async-start(), calls=%async_computation | async-start | bytes 524288 | tf_op jit(solution)/shard_map/psum | solution.py:99
  8.9 6.1 %collective-permute-start = (f32[128,169]{0,1:T(8,128)S(1)}, f32[128,169]{0,1:T(8,128)S(1)}, u32[]{:S(2)}, u32[]{:S(2)}) collective-permute-start(f32[128,169]{0,1:T(8,128)S(1)} %bitcast.162), channel_id=1, source_target_pairs={{2,0},{4,2},{6,4},{8,6},{10,8},{12,10},{14,12},{16,14},{18,16},{20... | collective-permute-start | bytes 259592 | tf_op jit(solution)/shard_map/ppermute | solution.py:13
  12.4 2.6 copy-start.1
  23.7 1.2 copy-start.3
  24.9 3.6 copy-start.7
  32.8 12.4 %copy-start.8 = (f32[2]{0:T(128)S(1)}, f32[2]{0:T(128)}, u32[]{:S(2)}) copy-start(f32[2]{0:T(128)} %param.21) | copy-start | bytes 28
  32.9 17.3 %copy-start.4 = (f32[676]{0:T(1024)S(1)}, f32[676]{0:T(1024)}, u32[]{:S(2)}) copy-start(f32[676]{0:T(1024)} %param.17) | copy-start | bytes 8116
  41.2 7.4 %collective-permute-start.1 = (f32[128,169]{0,1:T(8,128)S(1)}, f32[128,169]{0,1:T(8,128)S(1)}, u32[]{:S(2)}, u32[]{:S(2)}) collective-permute-start(f32[128,169]{0,1:T(8,128)S(1)} %slice.114), channel_id=1, source_target_pairs={{0,2},{2,4},{4,6},{6,8},{8,10},{10,12},{12,14},{14,16},{16,18},{18... | collective-permute-start | bytes 259592 | tf_op jit(solution)/shard_map/ppermute | solution.py:13
  51.0 5.3 %collective-permute-start.2 = (f32[128,169]{0,1:T(8,128)S(1)}, f32[128,169]{0,1:T(8,128)S(1)}, u32[]{:S(2)}, u32[]{:S(2)}) collective-permute-start(f32[128,169]{0,1:T(8,128)S(1)} %bitcast.164), channel_id=1, source_target_pairs={{2,0},{4,2},{6,4},{8,6},{10,8},{12,10},{14,12},{16,14},{18,16},{20... | collective-permute-start | bytes 259592 | tf_op jit(solution)/shard_map/ppermute | solution.py:13
  85.4 5.4 %collective-permute-start.3 = (f32[128,169]{0,1:T(8,128)S(1)}, f32[128,169]{0,1:T(8,128)S(1)}, u32[]{:S(2)}, u32[]{:S(2)}) collective-permute-start(f32[128,169]{0,1:T(8,128)S(1)} %slice.116), channel_id=1, source_target_pairs={{0,2},{2,4},{4,6},{6,8},{8,10},{10,12},{12,14},{14,16},{16,18},{18... | collective-permute-start | bytes 259592 | tf_op jit(solution)/shard_map/ppermute | solution.py:13
  93.2 5.9 %collective-permute-start.4 = (f32[128,169]{0,1:T(8,128)S(1)}, f32[128,169]{0,1:T(8,128)S(1)}, u32[]{:S(2)}, u32[]{:S(2)}) collective-permute-start(f32[128,169]{0,1:T(8,128)S(1)} %bitcast.165), channel_id=1, source_target_pairs={{2,0},{4,2},{6,4},{8,6},{10,8},{12,10},{14,12},{16,14},{18,16},{20... | collective-permute-start | bytes 259592 | tf_op jit(solution)/shard_map/ppermute | solution.py:13
  123.0 6.1 %collective-permute-start.5 = (f32[128,169]{0,1:T(8,128)S(1)}, f32[128,169]{0,1:T(8,128)S(1)}, u32[]{:S(2)}, u32[]{:S(2)}) collective-permute-start(f32[128,169]{0,1:T(8,128)S(1)} %slice.118), channel_id=1, source_target_pairs={{0,2},{2,4},{4,6},{6,8},{8,10},{10,12},{12,14},{14,16},{16,18},{18... | collective-permute-start | bytes 259592 | tf_op jit(solution)/shard_map/ppermute | solution.py:13
  131.6 5.6 %collective-permute-start.6 = (f32[128,169]{0,1:T(8,128)S(1)}, f32[128,169]{0,1:T(8,128)S(1)}, u32[]{:S(2)}, u32[]{:S(2)}) collective-permute-start(f32[128,169]{0,1:T(8,128)S(1)} %bitcast.163), channel_id=1, source_target_pairs={{2,0},{4,2},{6,4},{8,6},{10,8},{12,10},{14,12},{16,14},{18,16},{20... | collective-permute-start | bytes 259592 | tf_op jit(solution)/shard_map/ppermute | solution.py:13
  418.7 1.2 copy-start.2
  486.5 0.7 copy-start.9
Sparse Core Ops, SparseCore 0:
  158.9 259.7 all-reduce.2
where the time goes:
time: 512 us; the launch traced here: 503 us
  waiting for transfers between devices  276 us (54%)
  other arithmetic  94.8 us (19%)
  local copies, waits for them, and re-layouts  49.7 us (10%)
  blocking collectives  28 us (5%)
  matrix products  18.2 us (4%)
  between operations  18.2 us (4%)
  starting transfers between devices  18 us (4%)
    psum x1, waiting for transfers between devices, per_device(): gram = lax.psum(term, 'dom') / total_nodes  260 us
    another operation x6, other arithmetic, per_device(): multiplier = jnp.linalg.cholesky(gram)  34 us
    scatter-add x3, other arithmetic, cell_apply(): return jnp.zeros_like(ext).at[:, conn.reshape(-1)].add(values)  25 us
    another operation x3, other arithmetic, per_device(): jax.scipy.linalg.solve_triangular(multiplier, identity, lower=True)  19.7 us
    all_gather x1, blocking collectives, per_device(): whole = lax.all_gather(ext, 'orb', axis=0, tiled=True)  19.2 us
    ppermute x7, starting transfers between devices, shifted(): lax.ppermute(value, axis, [(source, source + steps) for source in range(i...  18 us
    ppermute x7, waiting for transfers between devices, shifted(): lax.ppermute(value, axis, [(source, source + steps) for source in range(i...  16.4 us
  transfers between devices with their start and end apart: 8, of which 7 were waited for; matrix products, arithmetic and copies ran while one was open for 1% of the time, Pallas kernels for 0%

commit v1 on v0

v1 whole, which is shorter than its diff:
```python
import functools

import jax
import jax.numpy as jnp
from jax import lax
from jax.experimental import pallas as pl
from jax.experimental.pallas import tpu as pltpu
from jax.sharding import Mesh
from jax.sharding import PartitionSpec as P

ORBS = 256
HALF = 128
DEG = 3
NPC = 125
GAUSS = 216
FACE = 169
OWN = 676
CELLS = 9
OWN_PAD = 680
FACE_PAD = 176
GHOST_AT = 768
EXT = 1024
PICK = CELLS * 128
ROWS = 1040
OCC_AT = OWN_PAD + FACE_PAD
FIELD = 864
VMEM = 24 * 1024 * 1024
F32 = jnp.float32
BF16 = jnp.bfloat16


def split(value):
    high = value.astype(BF16)
    return high, (value - high.astype(F32)).astype(BF16)


def dot(a, b, dims=((1,), (0,))):
    return lax.dot_general(a, b, (dims, ((), ())), preferred_element_type=F32)


def dot3(a, b, dims=((1,), (0,))):
    a_high, a_low = split(a)
    b_high, b_low = split(b)
    return dot(a_high, b_high, dims) + (dot(a_high, b_low, dims) + dot(a_low, b_high, dims))


def dot6(a, b, dims=((1,), (0,))):
    return lax.dot_general(
        a, b, (dims, ((), ())), precision=lax.Precision.HIGHEST, preferred_element_type=F32
    )


def put_split(ref, rows, value):
    high, low = split(value)
    ref[rows, 0:HALF] = high
    ref[rows, HALF : 2 * HALF] = low


def joined(value):
    return value[:, 0:HALF] + value[:, HALF : 2 * HALF]


def apply_cells(own, ghost, pick_ref, place_ref, matrix_ref, ext_ref, cell_ref, outs):
    ext_ref[OWN_PAD:GHOST_AT] = jnp.zeros((GHOST_AT - OWN_PAD, 2 * HALF), BF16)
    ext_ref[GHOST_AT + FACE_PAD : EXT] = jnp.zeros((EXT - GHOST_AT - FACE_PAD, 2 * HALF), BF16)
    put_split(ext_ref, slice(0, OWN_PAD), own)
    put_split(ext_ref, slice(GHOST_AT, GHOST_AT + FACE_PAD), ghost)
    picked = joined(dot(pick_ref[...], ext_ref[...]))
    for cell in range(CELLS):
        rows = slice(cell * 128, cell * 128 + 128)
        high, low = split(picked[rows])
        matrix_high, matrix_low = split(matrix_ref[rows])
        term = joined(dot(matrix_high, jnp.concatenate([high, low], axis=1)))
        put_split(cell_ref, rows, term + dot(matrix_low, high))
    total = joined(dot(place_ref[...], cell_ref[...]))
    own_out, ghost_out, bottom_out = outs
    own_out[...] = total[0:OWN_PAD]
    ghost_out[...] = total[OWN_PAD : OWN_PAD + FACE_PAD]
    bottom_out[...] = total[OWN_PAD + FACE_PAD : OWN_PAD + 2 * FACE_PAD]


def first_kernel(own, ghost, pick, place, matrix, own_out, ghost_out, bottom_out, ext, cell):
    outs = (own_out, ghost_out, bottom_out)
    apply_cells(own[...], ghost[...], pick, place, matrix, ext, cell, outs)


def next_values(step, refs):
    (beta, own_sum, ghost_sum, from_below, from_above, spread, own_scale, ghost_scale) = refs[:8]
    factor = 1.0 if step == 0 else 2.0
    high, low = split(from_below[...])
    arrived = dot(spread[...], high) + dot(spread[...], low)
    own = refs[8][...]
    ghost = refs[9][...]
    shift = beta[0]
    new_own = factor * (own_scale[...] * (own_sum[...] + arrived[0:OWN_PAD]) - shift * own)
    new_ghost = factor * (ghost_scale[...] * (ghost_sum[...] + from_above[...]) - shift * ghost)
    if step > 0:
        new_own = new_own - refs[10][...]
        new_ghost = new_ghost - refs[11][...]
    return new_own, new_ghost


def step_kernel(step, *refs):
    n = 10 if step == 0 else 12
    pick, place, matrix = refs[n : n + 3]
    new_own_out, new_ghost_out, own_out, ghost_out, bottom_out, ext, cell = refs[n + 3 :]
    own, ghost = next_values(step, refs)
    new_own_out[...] = own
    new_ghost_out[...] = ghost
    apply_cells(own, ghost, pick, place, matrix, ext, cell, (own_out, ghost_out, bottom_out))


def last_kernel(step, *refs):
    occ, out = refs[12:]
    own, ghost = next_values(step, refs)
    out[0:OWN_PAD] = own
    out[OWN_PAD:OCC_AT] = ghost
    out[OCC_AT:FIELD] = jnp.broadcast_to(occ[...], (FIELD - OCC_AT, HALF))


def eliminate(block):
    groups = HALF // 8
    rows = [block[8 * i : 8 * i + 8] for i in range(groups)]
    lane = lax.broadcasted_iota(jnp.int32, (1, HALF), 1)
    sub = lax.broadcasted_iota(jnp.int32, (8, 1), 0)
    for k in range(HALF):
        group, at = divmod(k, 8)
        row = rows[group][at : at + 1]
        pivot = jnp.where(lane == k, 1.0, row) * (1.0 / row[:, k : k + 1])
        for i in range(group, groups):
            new = jnp.where(lane == k, 0.0, rows[i]) - rows[i][:, k : k + 1] * pivot
            rows[i] = jnp.where(sub > at, new, rows[i]) if i == group else new
    done = jnp.concatenate(rows, axis=0)
    i = lax.broadcasted_iota(jnp.int32, (HALF, HALF), 0)
    j = lax.broadcasted_iota(jnp.int32, (HALF, HALF), 1)
    diagonal = jnp.sum(jnp.where(i == j, done, 0.0), axis=1, keepdims=True)
    lower = jnp.where(i > j, done, jnp.where(i == j, 1.0, 0.0))
    return lower * lax.rsqrt(diagonal)


def density_kernel(gram, field, pick, interp, out, inverse, work, ext, quad):
    work[...] = gram[0, 0:HALF]
    inverse[0:HALF, HALF:] = jnp.zeros((HALF, HALF), F32)

    def body(part, carry):
        block = eliminate(work[...])

        @pl.when(part == 0)
        def _():
            inverse[0:HALF, 0:HALF] = block
            side = dot6(gram[0, HALF:], block, ((1,), (1,)))
            inverse[HALF:, 0:HALF] = dot6(side, block)
            work[...] = gram[1, HALF:] - dot6(side, side, ((1,), (1,)))

        @pl.when(part == 1)
        def _():
            inverse[HALF:, HALF:] = block
            inverse[HALF:, 0:HALF] = -dot6(block, inverse[HALF:, 0:HALF])

        return carry

    ext[OWN_PAD:GHOST_AT] = jnp.zeros((GHOST_AT - OWN_PAD, 4 * HALF), BF16)
    ext[GHOST_AT + FACE_PAD : EXT] = jnp.zeros((EXT - GHOST_AT - FACE_PAD, 4 * HALF), BF16)
    for half in range(2):
        lanes = slice(half * HALF, half * HALF + HALF)
        low_lanes = slice(ORBS + half * HALF, ORBS + half * HALF + HALF)
        for rows, at in (
            (slice(0, OWN_PAD), slice(0, OWN_PAD)),
            (slice(GHOST_AT, GHOST_AT + FACE_PAD), slice(OWN_PAD, OCC_AT)),
        ):
            high, low = split(field[half, at])
            ext[rows, lanes] = high
            ext[rows, low_lanes] = low
    picked = dot(pick[...], ext[...])
    values = picked[:, 0:ORBS] + picked[:, ORBS:]
    for cell in range(CELLS):
        quad[cell] = dot3(interp[...], values[cell * 128 : cell * 128 + 128])
    lax.fori_loop(0, 2, body, 0)
    occ = jnp.concatenate([field[0, OCC_AT : OCC_AT + 1], field[1, OCC_AT : OCC_AT + 1]], axis=1)
    weights = occ * (1.0 / ORBS)
    inv_high, inv_low = split(inverse[...])
    for cell in range(CELLS):
        high, low = split(quad[cell])
        dims = ((1,), (1,))
        value = dot(high, inv_high, dims) + (dot(high, inv_low, dims) + dot(low, inv_high, dims))
        out[:, cell : cell + 1] = jnp.sum(value * value * weights, axis=1, keepdims=True)


def call(kernel, shapes, scratch, operands, scalars=0):
    out = [jax.ShapeDtypeStruct(shape, F32) for shape in shapes]
    in_vmem = pl.BlockSpec(memory_space=pltpu.VMEM)
    specs = [pl.BlockSpec(memory_space=pltpu.SMEM)] * scalars
    specs = specs + [in_vmem] * (len(operands) - scalars)
    return pl.pallas_call(
        kernel,
        out_shape=out,
        in_specs=specs,
        out_specs=[in_vmem] * len(out),
        scratch_shapes=scratch,
        compiler_params=pltpu.CompilerParams(vmem_limit_bytes=VMEM),
    )(*operands)


def gather_all(value, axes):
    count = lax.axis_size(axes)
    return lax.all_to_all(jnp.broadcast_to(value[None], (count,) + value.shape), axes, 0, 0)


def per_device(
    block, conn, bottom, cell_scale, potential, mass, stiffness, interp, occupancy, spectrum
):
    dom = ("x", "z", "y")
    count = lax.axis_size(dom)
    down = [(i + 1, i) for i in range(count - 1)]
    up = [(i, i + 1) for i in range(count - 1)]
    halfwidth = (spectrum[1] - spectrum[0]) / 2.0
    centre = (spectrum[1] + spectrum[0]) / 2.0

    own = jnp.pad(block.T, ((0, OWN_PAD - OWN), (0, 0)))
    masses = jnp.pad(jnp.take(mass, bottom), (0, 2 * HALF - FACE)).reshape(2, HALF)
    face = jnp.concatenate(
        [jnp.take(own, bottom, axis=0), masses, jnp.zeros((FACE_PAD - FACE - 2, HALF), F32)], axis=0
    )
    ghost = lax.ppermute(face, dom, down)
    ghost_mass = ghost[FACE : FACE + 2].reshape(-1)[:FACE_PAD]
    own_mass = jnp.pad(mass, (0, OWN_PAD - OWN))

    def inverse_mass(values, used):
        live = (jnp.arange(values.shape[0]) < used) & (values > 0.0)
        scale = jnp.where(live, 1.0 / (jnp.where(live, values, 1.0) * halfwidth), 0.0)
        return jnp.broadcast_to(scale[:, None], (values.shape[0], HALF))

    own_scale = inverse_mass(own_mass, OWN)
    ghost_scale = inverse_mass(ghost_mass, FACE)

    nodes = jnp.where(conn < OWN, conn, conn + (GHOST_AT - OWN))
    nodes = jnp.pad(nodes.T, ((0, 0), (0, 128 - NPC)), constant_values=-1).reshape(PICK)
    listed = jnp.pad(bottom, (0, FACE_PAD - FACE), constant_values=-2)
    targets = jnp.concatenate(
        [
            jnp.arange(OWN_PAD),
            GHOST_AT + jnp.arange(FACE_PAD),
            listed,
            jnp.full((ROWS - OWN_PAD - 2 * FACE_PAD,), -2),
        ]
    )
    pick = (nodes[:, None] == jnp.arange(EXT)[None, :]).astype(BF16)
    place = (targets[:, None] == nodes[None, :]).astype(BF16)
    spread = (jnp.arange(688)[:, None] == listed[None, :]).astype(BF16)

    wide = jnp.pad(interp, ((0, 0), (0, 128 - NPC)))
    weighted = (wide[:, None, :] * potential[:, :, None]).reshape(GAUSS, PICK)
    cells = dot6(weighted, wide, ((0,), (0,)))
    stiff = jnp.pad(stiffness, ((0, 128 - NPC), (0, 128 - NPC)))
    cells = cells + (cell_scale[:, None, None] * stiff[None]).reshape(PICK, 128)
    tables = (pick, place, cells)

    scratch = [pltpu.VMEM((EXT, 2 * HALF), BF16), pltpu.VMEM((PICK, 2 * HALF), BF16)]
    own_shape, face_shape = (OWN_PAD, HALF), (FACE_PAD, HALF)
    sums = call(
        first_kernel, [own_shape, face_shape, face_shape], scratch, (own, ghost) + tables
    )
    beta = (centre / halfwidth).reshape(1)
    last = ()
    for step in range(DEG):
        own_sum, ghost_sum, bottom_sum = sums
        from_above = lax.ppermute(bottom_sum, dom, down)
        from_below = lax.ppermute(ghost_sum, dom, up)
        operands = (beta, own_sum, ghost_sum, from_below, from_above, spread, own_scale)
        operands = operands + (ghost_scale, own, ghost) + last
        last = (own, ghost)
        if step < DEG - 1:
            own, ghost, *sums = call(
                functools.partial(step_kernel, step),
                [own_shape, face_shape, own_shape, face_shape, face_shape],
                scratch,
                operands + tables,
                1,
            )
    (field,) = call(
        functools.partial(last_kernel, DEG - 1),
        [(FIELD, HALF)],
        [],
        operands + (occupancy.reshape(1, HALF),),
        1,
    )
    whole = lax.all_gather(field, "orb", axis=0)

    weighted = field[:OWN_PAD] * own_mass[:, None]
    term = jnp.concatenate(
        [dot6(whole[half, :OWN_PAD], weighted, ((0,), (0,))) for half in range(2)], axis=0
    )
    planes = lax.axis_size("z") * lax.axis_size("y")
    term = term * (1.0 / (count * OWN))
    pieces = lax.all_to_all(term.reshape(planes, ORBS // planes, HALF), ("z", "y"), 0, 0)
    piece = jnp.sum(gather_all(jnp.sum(pieces, axis=0), "x"), axis=0)
    gram = gather_all(piece, ("orb", "z", "y")).reshape(2, ORBS, HALF)

    (density,) = call(
        density_kernel,
        [(GAUSS, CELLS)],
        [
            pltpu.VMEM((ORBS, ORBS), F32),
            pltpu.VMEM((HALF, HALF), F32),
            pltpu.VMEM((EXT, 4 * HALF), BF16),
            pltpu.VMEM((CELLS, GAUSS, ORBS), F32),
        ],
        (gram, whole, pick, wide),
    )
    return density


def solution(mesh):
    side = round(mesh.shape["dom"] ** (1.0 / 3.0))
    torus = Mesh(mesh.devices.reshape(side, side, side, 2), ("x", "z", "y", "orb"))
    dom = ("x", "z", "y")
    in_specs = (
        P("orb", dom),
        P(None, dom),
        P(dom),
        P(dom),
        P(None, dom),
        P(dom),
        P(),
        P(),
        P("orb"),
        P(),
    )
    return jax.shard_map(
        per_device, mesh=torus, in_specs=in_specs, out_specs=P(None, dom), check_vma=False
    )
```

time: 512 us -> 175 us (0.34); the launches traced: 503 us -> 175 us
  waiting for transfers between devices: 276 us -> 4.58 us
  other arithmetic: 94.8 us -> 5.9 us
  blocking collectives: 28 us -> 95.7 us
  local copies, waits for them, and re-layouts: 49.7 us -> 4.67 us
  Pallas kernels: 0 us -> 37.4 us
  between operations: 18.2 us -> 3.16 us
  matrix products: 18.2 us -> 3.99 us
    psum x1 -> x0, waiting for transfers between devices: 260 us -> none  [per_device(): gram = lax.psum(term, 'dom') / total_nodes]
    all_to_all x0 -> x3, blocking collectives: none -> 76.6 us  [the longest x2 42.9 us: gather_all(): lax.all_to_all(jnp.broadcast_to(value[None], (count,) + value.shape), axe...]
    another operation x9 -> x0, other arithmetic: 53.7 us -> none  [the longest x6 34 us: per_device(): multiplier = jnp.linalg.cholesky(gram)]
    pallas_call x0 -> x5, Pallas kernels: none -> 37.4 us  [call(): pl.pallas_call(kernel, out_shape=out, in_specs=specs, out_specs=[in_vmem]...]
    scatter-add x6 -> x0, other arithmetic: 29.7 us -> none  [the longest x3 25 us: cell_apply(): return jnp.zeros_like(ext).at[:, conn.reshape(-1)].add(values)]
    reshape x20 -> x2, local copies, waits for them, and re-layouts: 15.4 us -> 0.01 us  [the longest x1 0.01 us: per_device(): jnp.pad(jnp.take(mass, bottom), (0, 2 * HALF - FACE)).reshape(2, HALF)]
    dot_general x12 -> x3, matrix products: 16.8 us -> 3.99 us  [dot6(): lax.dot_general(a, b, (dims, ((), ())), precision=lax.Precision.HIGHEST,...]
    ppermute x7, waiting for transfers between devices: 16.4 us -> 4.58 us  [the longest x3 3.64 us: per_device(): from_below = lax.ppermute(ghost_sum, dom, up)]
  transfers between devices with their start and end apart: 8 -> 7, of which waited for: 7 -> 4; matrix products, arithmetic and copies ran while one was open for 1% -> 3% of each run, Pallas kernels for 0% -> 0%
where the time goes in v1:
time: 175 us
  blocking collectives  95.7 us (55%)
  Pallas kernels  37.4 us (21%)
  starting transfers between devices  19.3 us (11%)
  other arithmetic  5.9 us (3%)
  local copies, waits for them, and re-layouts  4.67 us (3%)
  waiting for transfers between devices  4.58 us (3%)
  matrix products  3.99 us (2%)
  between operations  3.16 us (2%)
    all_to_all x2, blocking collectives, gather_all(): lax.all_to_all(jnp.broadcast_to(value[None], (count,) + value.shape), axe...  42.9 us
    pallas_call x5, Pallas kernels, call(): pl.pallas_call(kernel, out_shape=out, in_specs=specs, out_specs=[in_vmem]...  37.4 us
    all_to_all x1, blocking collectives, per_device(): lax.all_to_all(term.reshape(planes, ORBS // planes, HALF), ('z', 'y'), 0, 0)  33.7 us
    all_gather x1, blocking collectives, per_device(): whole = lax.all_gather(field, 'orb', axis=0)  19 us
    ppermute x3, starting transfers between devices, per_device(): from_below = lax.ppermute(ghost_sum, dom, up)  14.1 us
    dot_general x3, matrix products, dot6(): lax.dot_general(a, b, (dims, ((), ())), precision=lax.Precision.HIGHEST,...  3.99 us
    ppermute x3, starting transfers between devices, per_device(): from_above = lax.ppermute(bottom_sum, dom, down)  3.88 us
    ppermute x3, waiting for transfers between devices, per_device(): from_below = lax.ppermute(ghost_sum, dom, up)  3.64 us
  transfers between devices with their start and end apart: 7, of which 4 were waited for; matrix products, arithmetic and copies ran while one was open for 3% of the time, Pallas kernels for 0%

profile of v1, /device:TPU:1, one launch (start us, length us, event | category | flops | bytes accessed | tf_op | source)
XLA Modules:
  0.0 174.7 jit_solution(1062937778936532118)
XLA Ops:
  1.4 1.9 %gather_fusion.1 = f32[169]{0:T(256)S(1)} fusion(f32[676]{0:T(1024)} %param.15, s32[1024]{0:T(1024)S(1)} %get-tuple-element.37), kind=kCustom, calls=%fused_computation.1 | custom fusion | bytes 2028 | tf_op jit(solution)/shard_map/jit(_take)/gather | solution.py:220
  3.4 0.7 and_select_fusion
  5.8 1.3 collective-permute-start
  11.4 1.9 %compare_convert_fusion.place.refs_11_.refs_13_ = bf16[1040,1152]{1,0:T(8,128)(2,1)} fusion(s32[1152]{0:T(1024)S(1)} %pad_bitcast_fusion, s32[1040]{0:T(1024)S(1)} %concatenate.10), kind=kLoop, calls=%fused_computation.2 | loop fusion | flops 2396160 | bytes 2404928 | tf_op jit(solution)/shard_map/convert_element_type | solution.py:248
  13.7 2.1 %convolution_add_fusion.matrix.refs_12_.refs_14_ = f32[1152,128]{1,0:T(8,128)S(1)} fusion(f32[1152,128]{1,0:T(8,128)S(1)} %bitcast_multiply_fusion, f32[216,1152]{0,1:T(8,128)S(1)} %bitcast.33, f32[216,125]{1,0:T(8,128)} %param.17), kind=kOutput, calls=%fused_computation.5 | convolution fusion | flops 382353408 | bytes 2282976 | tf_op jit(solution)/shard_map/dot_general | solution.py:48
  15.9 2.9 %shard_map.100 = (f32[680,128]{1,0:T(8,128)S(1)}, f32[176,128]{1,0:T(8,128)S(1)}, f32[176,128]{1,0:T(8,128)S(1)}) custom-call(f32[680,128]{1,0:T(8,128)S(1)} %pad.28.own.refs_8_.refs_10_, f32[176,128]{1,0:T(8,128)S(1)} %collective-permute-done.ghost.refs_9_.refs_11_, bf16[1152,1024]{1,0:T(8,128)(2,1)S(1)} %fusion.pick.refs_10_.refs_12_, ...), custom_call_target="tpu_custom_call" | custom-call | tf_op jit(solution)/shard_map/pallas_call | solution.py:194
  18.8 1.3 collective-permute-start.2
  20.1 5.4 %collective-permute-start.1 = (f32[176,128]{1,0:T(8,128)S(1)}, f32[176,128]{1,0:T(8,128)S(1)}, u32[]{:S(2)}, u32[]{:S(2)}) collective-permute-start(f32[176,128]{1,0:T(8,128)S(1)} %get-tuple-element.19.refs_2_), channel_id=1, source_target_pairs={{0,2},{2,4},{4,6},{6,8},{8,10},{10,12},{12,14},{14,16},{16,18},{18... | collective-permute-start | bytes 270344 | tf_op jit(solution)/shard_map/ppermute | solution.py:268
  25.5 0.9 collective-permute-done.2.refs_4_
  27.3 3.2 %shard_map.101 = (f32[680,128]{1,0:T(8,128)S(1)}, f32[176,128]{1,0:T(8,128)S(1)}, f32[680,128]{1,0:T(8,128)S(1)}, f32[176,128]{1,0:T(8,128)S(1)}, f32[176,128]{1,0:T(8,128)S(1)}) custom-call(f32[1]{0:T(128)} %bitcast.2.refs_0_, f32[680,128]{1,0:T(8,128)S(1)} %get-tuple-element.18.refs_1_, f32[176,128]{1,0:T(8,128)S(1)} %get-tuple-element.19.refs_2_, ...), custom_call_target="tpu_custom_call" | custom-call | tf_op jit(solution)/shard_map/pallas_call | solution.py:194
  30.5 1.3 collective-permute-start.4
  31.8 4.4 %collective-permute-start.3 = (f32[176,128]{1,0:T(8,128)S(1)}, f32[176,128]{1,0:T(8,128)S(1)}, u32[]{:S(2)}, u32[]{:S(2)}) collective-permute-start(f32[176,128]{1,0:T(8,128)S(1)} %get-tuple-element.22.refs_2_), channel_id=1, source_target_pairs={{0,2},{2,4},{4,6},{6,8},{8,10},{10,12},{12,14},{14,16},{16,18},{18... | collective-permute-start | bytes 270344 | tf_op jit(solution)/shard_map/ppermute | solution.py:268
  36.2 1.5 collective-permute-done.3.refs_3_
  37.8 3.3 %shard_map.102 = (f32[680,128]{1,0:T(8,128)S(1)}, f32[176,128]{1,0:T(8,128)S(1)}, f32[680,128]{1,0:T(8,128)S(1)}, f32[176,128]{1,0:T(8,128)S(1)}, f32[176,128]{1,0:T(8,128)S(1)}) custom-call(f32[1]{0:T(128)} %bitcast.2.refs_0_, f32[680,128]{1,0:T(8,128)S(1)} %get-tuple-element.21.refs_1_, f32[176,128]{1,0:T(8,128)S(1)} %get-tuple-element.22.refs_2_, ...), custom_call_target="tpu_custom_call" | custom-call | tf_op jit(solution)/shard_map/pallas_call | solution.py:194
  41.0 1.3 collective-permute-start.6
  42.3 4.4 %collective-permute-start.5 = (f32[176,128]{1,0:T(8,128)S(1)}, f32[176,128]{1,0:T(8,128)S(1)}, u32[]{:S(2)}, u32[]{:S(2)}) collective-permute-start(f32[176,128]{1,0:T(8,128)S(1)} %get-tuple-element.27.refs_2_), channel_id=1, source_target_pairs={{0,2},{2,4},{4,6},{6,8},{8,10},{10,12},{12,14},{14,16},{16,18},{18... | collective-permute-start | bytes 270344 | tf_op jit(solution)/shard_map/ppermute | solution.py:268
  46.7 1.5 collective-permute-done.5.refs_3_
  48.6 19.0 %all-gather = f32[1728,128]{1,0:T(8,128)S(1)} all-gather(f32[864,128]{1,0:T(8,128)S(1)} %shard_map.103), channel_id=2, replica_groups=mesh['x'=8,'z'=8,'y'=8,'orb'=2] {'orb'}, dimensions={0}, use_global_device_ids=true | all-gather | bytes 1327104 | tf_op jit(solution)/shard_map/all_gather | solution.py:287
  67.6 0.9 fusion.2
  68.6 0.9 fusion.3
  69.5 33.7 %all_to_all.15 = f32[64,4,128]{2,1,0:T(4,128)S(1)} all-to-all(f32[64,4,128]{2,1,0:T(4,128)S(1)} %bitcast.34), channel_id=1, replica_groups=mesh['x'=8,'z'=8,'y'=8,'orb'=2] {'z','y'}, dimensions={0} | all-to-all | bytes 262144 | tf_op jit(solution)/shard_map/all_to_all | solution.py:295
  103.3 19.0 %all_to_all.16 = f32[8,4,128]{2,1,0:T(4,128)S(1)} all-to-all(f32[8,4,128]{2,1,0:T(4,128)S(1)} %broadcast_in_dim.70), channel_id=1, replica_groups=mesh['x'=8,'z'=8,'y'=8,'orb'=2] {'x'}, dimensions={0} | all-to-all | bytes 32768 | tf_op jit(solution)/shard_map/all_to_all | solution.py:206
  122.4 23.9 %all_to_all.17 = f32[128,4,128]{2,1,0:T(4,128)S(1)} all-to-all(f32[128,4,128]{2,1,0:T(4,128)S(1)} %broadcast_in_dim.71), channel_id=1, replica_groups=mesh['x'=8,'z'=8,'y'=8,'orb'=2] {'orb','z','y'}, dimensions={0} | all-to-all | bytes 524288 | tf_op jit(solution)/shard_map/all_to_all | solution.py:206
  146.3 27.7 %shard_map.104 = f32[216,9]{1,0:T(8,128)S(1)} custom-call(f32[2,256,128]{2,1,0:T(8,128)S(1)} %bitcast.31, f32[2,864,128]{2,1,0:T(8,128)S(1)} %bitcast.30, bf16[1152,1024]{1,0:T(8,128)(2,1)S(1)} %fusion.pick.refs_10_.refs_12_, f32[216,128]{1,0:T(8,128)S(1)} %pad.32.interp), custom_call_target="tpu_custom_call" | custom-call | tf_op jit(solution)/shard_map/pallas_call | solution.py:194
  (64 shorter events, 6.9 us)
Async XLA Ops:
  0.0 10.5 %copy-start = (f32[9]{0:T(128)S(1)}, f32[9]{0:T(128)}, u32[]{:S(2)}) copy-start(f32[9]{0:T(128)} %param.13) | copy-start | bytes 112
  0.0 4.1 %copy-start.5 = (f32[128,676]{0,1:T(8,128)S(1)}, f32[128,676]{0,1:T(8,128)}, u32[]{:S(2)}) copy-start(f32[128,676]{0,1:T(8,128)} %param.10) | copy-start | bytes 1038340
  3.4 3.7 %copy-start.10 = (f32[2]{0:T(128)S(1)}, f32[2]{0:T(128)}, u32[]{:S(2)}) copy-start(f32[2]{0:T(128)} %param.19) | copy-start | bytes 28
  3.4 7.1 %copy-start.8 = (s32[169]{0:T(256)S(1)}, s32[169]{0:T(256)}, u32[]{:S(2)}) copy-start(s32[169]{0:T(256)} %param.12) | copy-start | bytes 2032
  3.4 7.1 %copy-start.9 = (s32[125,9]{0,1:T(8,128)S(1)}, s32[125,9]{0,1:T(8,128)}, u32[]{:S(2)}) copy-start(s32[125,9]{0,1:T(8,128)} %param.11) | copy-start | bytes 13504
  3.4 7.2 %copy-start.6 = (f32[125,125]{1,0:T(8,128)S(1)}, f32[125,125]{1,0:T(8,128)}, u32[]{:S(2)}) copy-start(f32[125,125]{1,0:T(8,128)} %param.16) | copy-start | bytes 187504
  3.4 7.2 %copy-start.4 = (f32[216,125]{1,0:T(8,128)S(1)}, f32[216,125]{1,0:T(8,128)}, u32[]{:S(2)}) copy-start(f32[216,125]{1,0:T(8,128)} %param.17) | copy-start | bytes 324004
  5.8 10.1 %collective-permute-start = (f32[176,128]{1,0:T(8,128)}, f32[176,128]{1,0:T(8,128)S(1)}, u32[]{:S(2)}, u32[]{:S(2)}) collective-permute-start(f32[176,128]{1,0:T(8,128)} %maximum_maximum_fusion), channel_id=1, source_target_pairs={{2,0},{4,2},{6,4},{8,6},{10,8},{12,10},{14,12},{16,14},{18,16},{20... | collective-permute-start | bytes 270344 | tf_op jit(solution)/shard_map/ppermute | solution.py:224
  11.4 2.2 %copy-start.7 = (f32[216,9]{0,1:T(8,128)S(1)}, f32[216,9]{0,1:T(8,128)}, u32[]{:S(2)}) copy-start(f32[216,9]{0,1:T(8,128)} %param.14) | copy-start | bytes 23332
  13.7 2.2 %copy-start.3 = (f32[676]{0:T(1024)S(1)}, f32[676]{0:T(1024)}, u32[]{:S(2)}) copy-start(f32[676]{0:T(1024)} %param.15) | copy-start | bytes 8116
  13.7 2.2 %copy-start.1 = (bf16[1040,1152]{1,0:T(8,128)(2,1)S(1)}, bf16[1040,1152]{1,0:T(8,128)(2,1)}, u32[]{:S(2)}) copy-start(bf16[1040,1152]{1,0:T(8,128)(2,1)} %compare_convert_fusion.place.refs_11_.refs_13_) | copy-start | bytes 7188484
  18.8 7.7 %collective-permute-start.2 = (f32[176,128]{1,0:T(8,128)S(1)}, f32[176,128]{1,0:T(8,128)S(1)}, u32[]{:S(2)}, u32[]{:S(2)}) collective-permute-start(f32[176,128]{1,0:T(8,128)S(1)} %get-tuple-element.20), channel_id=1, source_target_pairs={{2,0},{4,2},{6,4},{8,6},{10,8},{12,10},{14,12},{16,14},{18,16},{20... | collective-permute-start | bytes 270344 | tf_op jit(solution)/shard_map/ppermute | solution.py:267
  20.1 7.0 %collective-permute-start.1 = (f32[176,128]{1,0:T(8,128)S(1)}, f32[176,128]{1,0:T(8,128)S(1)}, u32[]{:S(2)}, u32[]{:S(2)}) collective-permute-start(f32[176,128]{1,0:T(8,128)S(1)} %get-tuple-element.19.refs_2_), channel_id=1, source_target_pairs={{0,2},{2,4},{4,6},{6,8},{8,10},{10,12},{12,14},{14,16},{16,18},{18... | collective-permute-start | bytes 270344 | tf_op jit(solution)/shard_map/ppermute | solution.py:268
  30.5 5.7 %collective-permute-start.4 = (f32[176,128]{1,0:T(8,128)S(1)}, f32[176,128]{1,0:T(8,128)S(1)}, u32[]{:S(2)}, u32[]{:S(2)}) collective-permute-start(f32[176,128]{1,0:T(8,128)S(1)} %get-tuple-element.23), channel_id=1, source_target_pairs={{2,0},{4,2},{6,4},{8,6},{10,8},{12,10},{14,12},{16,14},{18,16},{20... | collective-permute-start | bytes 270344 | tf_op jit(solution)/shard_map/ppermute | solution.py:267
  31.8 5.9 %collective-permute-start.3 = (f32[176,128]{1,0:T(8,128)S(1)}, f32[176,128]{1,0:T(8,128)S(1)}, u32[]{:S(2)}, u32[]{:S(2)}) collective-permute-start(f32[176,128]{1,0:T(8,128)S(1)} %get-tuple-element.22.refs_2_), channel_id=1, source_target_pairs={{0,2},{2,4},{4,6},{6,8},{8,10},{10,12},{12,14},{14,16},{16,18},{18... | collective-permute-start | bytes 270344 | tf_op jit(solution)/shard_map/ppermute | solution.py:268
  37.8 10.5 %copy-start.2 = (f32[128]{0:T(128)S(1)}, f32[128]{0:T(128)}, u32[]{:S(2)}) copy-start(f32[128]{0:T(128)} %param.18) | copy-start | bytes 1540
  41.0 5.7 %collective-permute-start.6 = (f32[176,128]{1,0:T(8,128)S(1)}, f32[176,128]{1,0:T(8,128)S(1)}, u32[]{:S(2)}, u32[]{:S(2)}) collective-permute-start(f32[176,128]{1,0:T(8,128)S(1)} %get-tuple-element.28), channel_id=1, source_target_pairs={{2,0},{4,2},{6,4},{8,6},{10,8},{12,10},{14,12},{16,14},{18,16},{20... | collective-permute-start | bytes 270344 | tf_op jit(solution)/shard_map/ppermute | solution.py:267
  42.3 5.9 %collective-permute-start.5 = (f32[176,128]{1,0:T(8,128)S(1)}, f32[176,128]{1,0:T(8,128)S(1)}, u32[]{:S(2)}, u32[]{:S(2)}) collective-permute-start(f32[176,128]{1,0:T(8,128)S(1)} %get-tuple-element.27.refs_2_), channel_id=1, source_target_pairs={{0,2},{2,4},{4,6},{6,8},{8,10},{10,12},{12,14},{14,16},{16,18},{18... | collective-permute-start | bytes 270344 | tf_op jit(solution)/shard_map/ppermute | solution.py:268

commit v2 on v1

--- a/solution.py
+++ b/solution.py
@@ -118,24 +118,46 @@
     out[OCC_AT:FIELD] = jnp.broadcast_to(occ[...], (FIELD - OCC_AT, HALF))
 
 
+def reciprocal(value):
+    guess = pl.reciprocal(value, approx=True)
+    guess = guess * (2.0 - value * guess)
+    return guess * (2.0 - value * guess)
+
+
 def eliminate(block):
     groups = HALF // 8
     rows = [block[8 * i : 8 * i + 8] for i in range(groups)]
     lane = lax.broadcasted_iota(jnp.int32, (1, HALF), 1)
     sub = lax.broadcasted_iota(jnp.int32, (8, 1), 0)
-    for k in range(HALF):
+    for k in range(0, HALF, 2):
         group, at = divmod(k, 8)
-        row = rows[group][at : at + 1]
-        pivot = jnp.where(lane == k, 1.0, row) * (1.0 / row[:, k : k + 1])
+        left = [jnp.broadcast_to(rows[i][:, k : k + 1], (8, HALF)) for i in range(group, groups)]
+        right = [
+            jnp.broadcast_to(rows[i][:, k + 1 : k + 2], (8, HALF)) for i in range(group, groups)
+        ]
+        a = left[0][at : at + 1]
+        b = left[0][at + 1 : at + 2]
+        d = right[0][at + 1 : at + 2]
+        scale = reciprocal(a * d - b * b)
+        here, beside = lane == k, lane == k + 1
+        upper = jnp.where(here, 1.0, jnp.where(beside, 0.0, rows[group][at : at + 1]))
+        under = jnp.where(here, 0.0, jnp.where(beside, 1.0, rows[group][at + 1 : at + 2]))
+        first = (d * upper - b * under) * scale
+        second = (a * under - b * upper) * scale
         for i in range(group, groups):
-            new = jnp.where(lane == k, 0.0, rows[i]) - rows[i][:, k : k + 1] * pivot
-            rows[i] = jnp.where(sub > at, new, rows[i]) if i == group else new
+            new = jnp.where(here | beside, 0.0, rows[i])
+            new = new - left[i - group] * first - right[i - group] * second
+            rows[i] = jnp.where(sub > at + 1, new, rows[i]) if i == group else new
     done = jnp.concatenate(rows, axis=0)
     i = lax.broadcasted_iota(jnp.int32, (HALF, HALF), 0)
     j = lax.broadcasted_iota(jnp.int32, (HALF, HALF), 1)
+    odd = lax.broadcasted_iota(jnp.int32, (HALF, 1), 0) % 2 == 1
     diagonal = jnp.sum(jnp.where(i == j, done, 0.0), axis=1, keepdims=True)
-    lower = jnp.where(i > j, done, jnp.where(i == j, 1.0, 0.0))
-    return lower * lax.rsqrt(diagonal)
+    below = jnp.sum(jnp.where(i == j + 1, done, 0.0), axis=1, keepdims=True)
+    lower = jnp.where(i // 2 > j // 2, done, jnp.where(i == j, 1.0, 0.0))
+    ratio = jnp.where(odd, below / pltpu.roll(diagonal, 1, 0), 0.0)
+    lower = lower - ratio * pltpu.roll(lower, 1, 0)
+    return lower * lax.rsqrt(diagonal - ratio * below)
 
 
 def density_kernel(gram, field, pick, interp, out, inverse, work, ext, quad):
@@ -209,7 +231,7 @@
 def per_device(
     block, conn, bottom, cell_scale, potential, mass, stiffness, interp, occupancy, spectrum
 ):
-    dom = ("x", "z", "y")
+    dom = ("x", "zh", "zl", "y")
     count = lax.axis_size(dom)
     down = [(i + 1, i) for i in range(count - 1)]
     up = [(i, i + 1) for i in range(count - 1)]
@@ -290,11 +312,12 @@
     term = jnp.concatenate(
         [dot6(whole[half, :OWN_PAD], weighted, ((0,), (0,))) for half in range(2)], axis=0
     )
-    planes = lax.axis_size("z") * lax.axis_size("y")
+    near, far = ("zl", "y"), ("x", "zh")
+    size = lax.axis_size(near)
     term = term * (1.0 / (count * OWN))
-    pieces = lax.all_to_all(term.reshape(planes, ORBS // planes, HALF), ("z", "y"), 0, 0)
-    piece = jnp.sum(gather_all(jnp.sum(pieces, axis=0), "x"), axis=0)
-    gram = gather_all(piece, ("orb", "z", "y")).reshape(2, ORBS, HALF)
+    pieces = lax.all_to_all(term.reshape(size, ORBS // size, HALF), near, 0, 0)
+    piece = jnp.sum(gather_all(jnp.sum(pieces, axis=0), far), axis=0)
+    gram = lax.all_gather(gather_all(piece, near).reshape(ORBS, HALF), "orb", axis=0)
 
     (density,) = call(
         density_kernel,
@@ -312,8 +335,9 @@
 
 def solution(mesh):
     side = round(mesh.shape["dom"] ** (1.0 / 3.0))
-    torus = Mesh(mesh.devices.reshape(side, side, side, 2), ("x", "z", "y", "orb"))
-    dom = ("x", "z", "y")
+    shape = (side, side // 2, 2, side, 2)
+    torus = Mesh(mesh.devices.reshape(shape), ("x", "zh", "zl", "y", "orb"))
+    dom = ("x", "zh", "zl", "y")
     in_specs = (
         P("orb", dom),
         P(None, dom),

time: 175 us -> 164 us (0.937)
  Pallas kernels: 37.4 us -> 30.6 us
  blocking collectives: 95.7 us -> 89.2 us
    all_to_all x1, blocking collectives: 33.7 us -> 17.5 us  [per_device(): pieces = lax.all_to_all(term.reshape(size, ORBS // size, HALF), near, 0, 0)]
    pallas_call x5, Pallas kernels: 37.4 us -> 30.6 us  [call(): pl.pallas_call(kernel, out_shape=out, in_specs=specs, out_specs=[in_vmem]...]
    all_gather x0 -> x1, blocking collectives: none -> 5.7 us  [per_device(): lax.all_gather(gather_all(piece, near).reshape(ORBS, HALF), 'orb', axis=0)]
    all_to_all x2, blocking collectives: 42.9 us -> 47 us  [gather_all(): lax.all_to_all(jnp.broadcast_to(value[None], (count,) + value.shape), axe...]
  transfers between devices with their start and end apart: 7 -> 7, of which waited for: 4 -> 4; matrix products, arithmetic and copies ran while one was open for 3% -> 4% of each run, Pallas kernels for 0% -> 0%
where the time goes in v2:
time: 164 us; the launch traced here: 163 us
  blocking collectives  89.2 us (54%)
  Pallas kernels  30.6 us (19%)
  starting transfers between devices  19.3 us (12%)
  other arithmetic  7.64 us (5%)
  local copies, waits for them, and re-layouts  5.81 us (4%)
  waiting for transfers between devices  4.58 us (3%)
  between operations  3.14 us (2%)
  matrix products  2.92 us (2%)
    all_to_all x2, blocking collectives, gather_all(): lax.all_to_all(jnp.broadcast_to(value[None], (count,) + value.shape), axe...  47 us
    pallas_call x5, Pallas kernels, call(): pl.pallas_call(kernel, out_shape=out, in_specs=specs, out_specs=[in_vmem]...  30.6 us
    all_gather x1, blocking collectives, per_device(): whole = lax.all_gather(field, 'orb', axis=0)  19 us
    all_to_all x1, blocking collectives, per_device(): pieces = lax.all_to_all(term.reshape(size, ORBS // size, HALF), near, 0, 0)  17.5 us
    ppermute x3, starting transfers between devices, per_device(): from_below = lax.ppermute(ghost_sum, dom, up)  14.1 us
    all_gather x1, blocking collectives, per_device(): lax.all_gather(gather_all(piece, near).reshape(ORBS, HALF), 'orb', axis=0)  5.7 us
    ppermute x3, waiting for transfers between devices, per_device(): from_below = lax.ppermute(ghost_sum, dom, up)  4.22 us
    ppermute x3, starting transfers between devices, per_device(): from_above = lax.ppermute(bottom_sum, dom, down)  3.88 us
  transfers between devices with their start and end apart: 7, of which 4 were waited for; matrix products, arithmetic and copies ran while one was open for 4% of the time, Pallas kernels for 0%

profile of v2, /device:TPU:1, one launch (start us, length us, event | category | flops | bytes accessed | tf_op | source)
XLA Modules:
  0.0 163.2 jit_solution(6776199179961859683)
XLA Ops:
  1.4 1.9 %gather_fusion.1 = f32[169]{0:T(256)S(1)} fusion(f32[676]{0:T(1024)} %param.15, s32[1024]{0:T(1024)S(1)} %get-tuple-element.37), kind=kCustom, calls=%fused_computation.1 | custom fusion | bytes 2028 | tf_op jit(solution)/shard_map/jit(_take)/gather | solution.py:242
  5.8 1.3 collective-permute-start
  12.0 1.9 %compare_convert_fusion.place.refs_11_.refs_13_ = bf16[1040,1152]{1,0:T(8,128)(2,1)} fusion(s32[1152]{0:T(1024)S(1)} %pad_bitcast_fusion, s32[1040]{0:T(1024)S(1)} %concatenate.10), kind=kLoop, calls=%fused_computation.2 | loop fusion | flops 2396160 | bytes 2404928 | tf_op jit(solution)/shard_map/convert_element_type | solution.py:270
  14.0 1.1 bitcast_multiply_fusion
  15.2 1.1 convolution_add_fusion.matrix.refs_12_.refs_14_
  16.8 2.9 %shard_map.100 = (f32[680,128]{1,0:T(8,128)S(1)}, f32[176,128]{1,0:T(8,128)S(1)}, f32[176,128]{1,0:T(8,128)S(1)}) custom-call(f32[680,128]{1,0:T(8,128)S(1)} %pad.28.own.refs_8_.refs_10_, f32[176,128]{1,0:T(8,128)S(1)} %collective-permute-done.ghost.refs_9_.refs_11_, bf16[1152,1024]{1,0:T(8,128)(2,1)S(1)} %fusion.pick.refs_10_.refs_12_, ...), custom_call_target="tpu_custom_call" | custom-call | tf_op jit(solution)/shard_map/pallas_call | solution.py:216
  19.7 1.3 collective-permute-start.2
  21.0 5.4 %collective-permute-start.1 = (f32[176,128]{1,0:T(8,128)S(1)}, f32[176,128]{1,0:T(8,128)S(1)}, u32[]{:S(2)}, u32[]{:S(2)}) collective-permute-start(f32[176,128]{1,0:T(8,128)S(1)} %get-tuple-element.19.refs_2_), channel_id=1, source_target_pairs={{0,2},{2,4},{4,6},{6,8},{8,10},{10,12},{12,14},{14,16},{16,18},{18... | collective-permute-start | bytes 270344 | tf_op jit(solution)/shard_map/ppermute | solution.py:290
  26.8 1.2 collective-permute-done.1.refs_3_
  28.2 3.2 %shard_map.101 = (f32[680,128]{1,0:T(8,128)S(1)}, f32[176,128]{1,0:T(8,128)S(1)}, f32[680,128]{1,0:T(8,128)S(1)}, f32[176,128]{1,0:T(8,128)S(1)}, f32[176,128]{1,0:T(8,128)S(1)}) custom-call(f32[1]{0:T(128)} %bitcast.2.refs_0_, f32[680,128]{1,0:T(8,128)S(1)} %get-tuple-element.18.refs_1_, f32[176,128]{1,0:T(8,128)S(1)} %get-tuple-element.19.refs_2_, ...), custom_call_target="tpu_custom_call" | custom-call | tf_op jit(solution)/shard_map/pallas_call | solution.py:216
  31.5 1.3 collective-permute-start.4
  32.8 4.4 %collective-permute-start.3 = (f32[176,128]{1,0:T(8,128)S(1)}, f32[176,128]{1,0:T(8,128)S(1)}, u32[]{:S(2)}, u32[]{:S(2)}) collective-permute-start(f32[176,128]{1,0:T(8,128)S(1)} %get-tuple-element.22.refs_2_), channel_id=1, source_target_pairs={{0,2},{2,4},{4,6},{6,8},{8,10},{10,12},{12,14},{14,16},{16,18},{18... | collective-permute-start | bytes 270344 | tf_op jit(solution)/shard_map/ppermute | solution.py:290
  37.1 1.5 collective-permute-done.3.refs_3_
  38.7 3.3 %shard_map.102 = (f32[680,128]{1,0:T(8,128)S(1)}, f32[176,128]{1,0:T(8,128)S(1)}, f32[680,128]{1,0:T(8,128)S(1)}, f32[176,128]{1,0:T(8,128)S(1)}, f32[176,128]{1,0:T(8,128)S(1)}) custom-call(f32[1]{0:T(128)} %bitcast.2.refs_0_, f32[680,128]{1,0:T(8,128)S(1)} %get-tuple-element.21.refs_1_, f32[176,128]{1,0:T(8,128)S(1)} %get-tuple-element.22.refs_2_, ...), custom_call_target="tpu_custom_call" | custom-call | tf_op jit(solution)/shard_map/pallas_call | solution.py:216
  42.0 1.3 collective-permute-start.6
  43.3 4.3 %collective-permute-start.5 = (f32[176,128]{1,0:T(8,128)S(1)}, f32[176,128]{1,0:T(8,128)S(1)}, u32[]{:S(2)}, u32[]{:S(2)}) collective-permute-start(f32[176,128]{1,0:T(8,128)S(1)} %get-tuple-element.27.refs_2_), channel_id=1, source_target_pairs={{0,2},{2,4},{4,6},{6,8},{8,10},{10,12},{12,14},{14,16},{16,18},{18... | collective-permute-start | bytes 270344 | tf_op jit(solution)/shard_map/ppermute | solution.py:290
  47.6 1.5 collective-permute-done.5.refs_3_
  49.5 19.0 %all-gather = f32[1728,128]{1,0:T(8,128)S(1)} all-gather(f32[864,128]{1,0:T(8,128)S(1)} %shard_map.103), channel_id=2, replica_groups=mesh['x'=8,'zh'=4,'zl'=2,'y'=8,'orb'=2] {'orb'}, dimensions={0}, use_global_device_ids=true | all-gather | bytes 1327104 | tf_op jit(solution)/shard_map/all_gather | solution.py:309
  70.4 17.5 %all_to_all.15 = f32[16,16,128]{2,1,0:T(8,128)S(1)} all-to-all(f32[16,16,128]{2,1,0:T(8,128)S(1)} %bitcast.34), channel_id=1, replica_groups=mesh['x'=8,'zh'=4,'zl'=2,'y'=8,'orb'=2] {'zl','y'}, dimensions={0} | all-to-all | bytes 262144 | tf_op jit(solution)/shard_map/all_to_all | solution.py:318
  88.0 35.4 %all_to_all.16 = f32[32,16,128]{2,1,0:T(8,128)} all-to-all(f32[32,16,128]{2,1,0:T(8,128)S(1)} %broadcast_in_dim.70), channel_id=1, replica_groups=mesh['x'=8,'zh'=4,'zl'=2,'y'=8,'orb'=2] {'x','zh'}, dimensions={0} | all-to-all | bytes 524288 | tf_op jit(solution)/shard_map/all_to_all | solution.py:228
  123.4 1.0 reduce_sum.19
  124.4 11.6 %all_to_all.17 = f32[16,16,128]{2,1,0:T(8,128)S(1)} all-to-all(f32[16,16,128]{2,1,0:T(8,128)S(1)} %broadcast_in_dim.71), channel_id=1, replica_groups=mesh['x'=8,'zh'=4,'zl'=2,'y'=8,'orb'=2] {'zl','y'}, dimensions={0} | all-to-all | bytes 262144 | tf_op jit(solution)/shard_map/all_to_all | solution.py:228
  136.0 5.7 %all_gather.11.gram = f32[2,256,128]{2,1,0:T(8,128)S(1)} all-gather(f32[1,256,128]{2,1,0:T(8,128)S(1)} %bitcast.33), channel_id=1, replica_groups=mesh['x'=8,'zh'=4,'zl'=2,'y'=8,'orb'=2] {'orb'}, dimensions={0}, use_global_device_ids=true | all-gather | bytes 393216 | tf_op jit(solution)/shard_map/all_gather | solution.py:320
  141.7 20.8 %shard_map.104 = f32[216,9]{1,0:T(8,128)S(1)} custom-call(f32[2,256,128]{2,1,0:T(8,128)S(1)} %all_gather.11.gram, f32[2,864,128]{2,1,0:T(8,128)S(1)} %bitcast.30, bf16[1152,1024]{1,0:T(8,128)(2,1)S(1)} %fusion.pick.refs_10_.refs_12_, f32[216,128]{1,0:T(8,128)S(1)} %pad.32.interp), custom_call_target="tpu_custom_call" | custom-call | tf_op jit(solution)/shard_map/pallas_call | solution.py:216
  (65 shorter events, 10.1 us)
Async XLA Ops:
  0.0 10.5 %copy-start = (f32[9]{0:T(128)S(1)}, f32[9]{0:T(128)}, u32[]{:S(2)}) copy-start(f32[9]{0:T(128)} %param.13) | copy-start | bytes 112
  0.0 4.1 %copy-start.5 = (f32[128,676]{0,1:T(8,128)S(1)}, f32[128,676]{0,1:T(8,128)}, u32[]{:S(2)}) copy-start(f32[128,676]{0,1:T(8,128)} %param.10) | copy-start | bytes 1038340
  3.4 3.7 %copy-start.10 = (f32[2]{0:T(128)S(1)}, f32[2]{0:T(128)}, u32[]{:S(2)}) copy-start(f32[2]{0:T(128)} %param.19) | copy-start | bytes 28
  3.4 7.1 %copy-start.8 = (s32[169]{0:T(256)S(1)}, s32[169]{0:T(256)}, u32[]{:S(2)}) copy-start(s32[169]{0:T(256)} %param.12) | copy-start | bytes 2032
  3.4 7.1 %copy-start.9 = (s32[125,9]{0,1:T(8,128)S(1)}, s32[125,9]{0,1:T(8,128)}, u32[]{:S(2)}) copy-start(s32[125,9]{0,1:T(8,128)} %param.11) | copy-start | bytes 13504
  3.4 7.2 %copy-start.6 = (f32[125,125]{1,0:T(8,128)S(1)}, f32[125,125]{1,0:T(8,128)}, u32[]{:S(2)}) copy-start(f32[125,125]{1,0:T(8,128)} %param.16) | copy-start | bytes 187504
  3.4 7.8 %copy-start.4 = (f32[216,125]{1,0:T(8,128)S(1)}, f32[216,125]{1,0:T(8,128)}, u32[]{:S(2)}) copy-start(f32[216,125]{1,0:T(8,128)} %param.17) | copy-start | bytes 324004
  5.8 10.5 %collective-permute-start = (f32[176,128]{1,0:T(8,128)}, f32[176,128]{1,0:T(8,128)S(1)}, u32[]{:S(2)}, u32[]{:S(2)}) collective-permute-start(f32[176,128]{1,0:T(8,128)} %maximum_maximum_fusion), channel_id=1, source_target_pairs={{2,0},{4,2},{6,4},{8,6},{10,8},{12,10},{14,12},{16,14},{18,16},{20... | collective-permute-start | bytes 270344 | tf_op jit(solution)/shard_map/ppermute | solution.py:246
  12.0 3.0 %copy-start.7 = (f32[216,9]{0,1:T(8,128)S(1)}, f32[216,9]{0,1:T(8,128)}, u32[]{:S(2)}) copy-start(f32[216,9]{0,1:T(8,128)} %param.14) | copy-start | bytes 23332
  15.1 1.1 copy-start.3
  15.2 1.7 %copy-start.1 = (bf16[1040,1152]{1,0:T(8,128)(2,1)S(1)}, bf16[1040,1152]{1,0:T(8,128)(2,1)}, u32[]{:S(2)}) copy-start(bf16[1040,1152]{1,0:T(8,128)(2,1)} %compare_convert_fusion.place.refs_11_.refs_13_) | copy-start | bytes 7188484
  19.7 7.1 %collective-permute-start.2 = (f32[176,128]{1,0:T(8,128)S(1)}, f32[176,128]{1,0:T(8,128)S(1)}, u32[]{:S(2)}, u32[]{:S(2)}) collective-permute-start(f32[176,128]{1,0:T(8,128)S(1)} %get-tuple-element.20), channel_id=1, source_target_pairs={{2,0},{4,2},{6,4},{8,6},{10,8},{12,10},{14,12},{16,14},{18,16},{20... | collective-permute-start | bytes 270344 | tf_op jit(solution)/shard_map/ppermute | solution.py:289
  21.0 7.0 %collective-permute-start.1 = (f32[176,128]{1,0:T(8,128)S(1)}, f32[176,128]{1,0:T(8,128)S(1)}, u32[]{:S(2)}, u32[]{:S(2)}) collective-permute-start(f32[176,128]{1,0:T(8,128)S(1)} %get-tuple-element.19.refs_2_), channel_id=1, source_target_pairs={{0,2},{2,4},{4,6},{6,8},{8,10},{10,12},{12,14},{14,16},{16,18},{18... | collective-permute-start | bytes 270344 | tf_op jit(solution)/shard_map/ppermute | solution.py:290
  31.5 5.7 %collective-permute-start.4 = (f32[176,128]{1,0:T(8,128)S(1)}, f32[176,128]{1,0:T(8,128)S(1)}, u32[]{:S(2)}, u32[]{:S(2)}) collective-permute-start(f32[176,128]{1,0:T(8,128)S(1)} %get-tuple-element.23), channel_id=1, source_target_pairs={{2,0},{4,2},{6,4},{8,6},{10,8},{12,10},{14,12},{16,14},{18,16},{20... | collective-permute-start | bytes 270344 | tf_op jit(solution)/shard_map/ppermute | solution.py:289
  32.8 5.9 %collective-permute-start.3 = (f32[176,128]{1,0:T(8,128)S(1)}, f32[176,128]{1,0:T(8,128)S(1)}, u32[]{:S(2)}, u32[]{:S(2)}) collective-permute-start(f32[176,128]{1,0:T(8,128)S(1)} %get-tuple-element.22.refs_2_), channel_id=1, source_target_pairs={{0,2},{2,4},{4,6},{6,8},{8,10},{10,12},{12,14},{14,16},{16,18},{18... | collective-permute-start | bytes 270344 | tf_op jit(solution)/shard_map/ppermute | solution.py:290
  38.7 10.5 %copy-start.2 = (f32[128]{0:T(128)S(1)}, f32[128]{0:T(128)}, u32[]{:S(2)}) copy-start(f32[128]{0:T(128)} %param.18) | copy-start | bytes 1540
  42.0 5.7 %collective-permute-start.6 = (f32[176,128]{1,0:T(8,128)S(1)}, f32[176,128]{1,0:T(8,128)S(1)}, u32[]{:S(2)}, u32[]{:S(2)}) collective-permute-start(f32[176,128]{1,0:T(8,128)S(1)} %get-tuple-element.28), channel_id=1, source_target_pairs={{2,0},{4,2},{6,4},{8,6},{10,8},{12,10},{14,12},{16,14},{18,16},{20... | collective-permute-start | bytes 270344 | tf_op jit(solution)/shard_map/ppermute | solution.py:289
  43.3 5.9 %collective-permute-start.5 = (f32[176,128]{1,0:T(8,128)S(1)}, f32[176,128]{1,0:T(8,128)S(1)}, u32[]{:S(2)}, u32[]{:S(2)}) collective-permute-start(f32[176,128]{1,0:T(8,128)S(1)} %get-tuple-element.27.refs_2_), channel_id=1, source_target_pairs={{0,2},{2,4},{4,6},{6,8},{8,10},{10,12},{12,14},{14,16},{16,18},{18... | collective-permute-start | bytes 270344 | tf_op jit(solution)/shard_map/ppermute | solution.py:290

commit v3 on v2

--- a/solution.py
+++ b/solution.py
@@ -24,6 +24,7 @@
 ROWS = 1040
 OCC_AT = OWN_PAD + FACE_PAD
 FIELD = 864
+DOM = ("xh", "xl", "zh", "zm", "zl", "yh", "yl")
 VMEM = 24 * 1024 * 1024
 F32 = jnp.float32
 BF16 = jnp.bfloat16
@@ -79,19 +80,140 @@
     bottom_out[...] = total[OWN_PAD + FACE_PAD : OWN_PAD + 2 * FACE_PAD]
 
 
-def first_kernel(own, ghost, pick, place, matrix, own_out, ghost_out, bottom_out, ext, cell):
+def column(row):
+    return jnp.broadcast_to(row, (HALF, HALF)).T
+
+
+def one_hot(left, right):
+    return jnp.where(left == right, 1.0, 0.0).astype(BF16)
+
+
+def face_kernel(block, bottom, mass, face, own, spread, listed, terms, select, ext):
+    own[0:OWN] = block[...]
+    own[OWN:OWN_PAD] = jnp.zeros((OWN_PAD - OWN, HALF), F32)
+    ext[OWN_PAD:GHOST_AT] = jnp.zeros((GHOST_AT - OWN_PAD, 2 * HALF), BF16)
+    put_split(ext, slice(0, OWN_PAD), own[...])
+    listed[...] = jnp.full(listed.shape, -2.0, F32)
+    listed[0:1, 0:FACE] = bottom[...].astype(F32)
+    lane = lax.broadcasted_iota(jnp.int32, (1, HALF), 1).astype(F32)
+    for at in range(0, FACE_PAD, HALF):
+        size = min(HALF, FACE_PAD - at)
+        wanted = column(listed[0:1, at : at + HALF])[0:size]
+        for start in range(0, GHOST_AT, HALF):
+            select[at : at + size, start : start + HALF] = one_hot(wanted, lane + float(start))
+    node = lax.broadcasted_iota(jnp.int32, (GHOST_AT, 2 * HALF), 0).astype(F32)
+    spread[...] = one_hot(node, listed[0:1])
+    terms[...] = jnp.zeros(terms.shape, F32)
+    terms[0:1, 0:OWN] = mass[...]
+    rest = terms[0:1]
+    for term in range(3):
+        part = rest.astype(BF16).astype(F32)
+        terms[term : term + 1] = part
+        rest = rest - part
+    parts = dot(terms[...].astype(BF16), spread[...])
+    masses = parts[0:1] + (parts[1:2] + parts[2:3])
+    face[...] = joined(dot(select[...], ext[...]))
+    face[FACE : FACE + 1] = masses[:, 0:HALF]
+    face[FACE + 1 : FACE + 2] = masses[:, HALF:]
+
+
+def halfwidth_of(spectrum):
+    low = jnp.full((1, HALF), spectrum[0], F32)
+    high = jnp.full((1, HALF), spectrum[1], F32)
+    return (high - low) * 0.5, (high + low) * 0.5
+
+
+def table_kernel(
+    spectrum,
+    scales,
+    conn,
+    bottom,
+    interp,
+    potential,
+    stiffness,
+    mass,
+    pick,
+    place,
+    matrix,
+    own_scale,
+    wide,
+    nodes,
+    listed,
+    targets,
+    square,
+    points,
+    weight,
+    masses,
+):
+    nodes[...] = jnp.full(nodes.shape, -1.0, F32)
+    own_node = conn[...] < OWN
+    named = jnp.where(own_node, conn[...], conn[...] + (GHOST_AT - OWN))
+    nodes[0:CELLS, 0:NPC] = named.astype(F32)
+    listed[...] = jnp.full(listed.shape, -2.0, F32)
+    listed[0:1, 0:FACE] = bottom[...].astype(F32)
+    lane = lax.broadcasted_iota(jnp.int32, (1, HALF), 1).astype(F32)
+    targets[...] = jnp.full(targets.shape, -2.0, F32)
+    row = lax.broadcasted_iota(jnp.int32, (OWN_PAD, HALF), 0).astype(F32)
+    targets[0:OWN_PAD] = row
+    targets[OWN_PAD:OCC_AT] = row[0:FACE_PAD] + float(GHOST_AT)
+    for at in range(0, FACE_PAD, HALF):
+        size = min(HALF, FACE_PAD - at)
+        targets[OCC_AT + at : OCC_AT + at + size] = column(listed[0:1, at : at + HALF])[0:size]
+    square[...] = jnp.zeros(square.shape, F32)
+    square[0:NPC, 0:NPC] = stiffness[...]
+    points[...] = jnp.zeros(points.shape, F32)
+    points[0:GAUSS, 0:NPC] = interp[...]
+    wide[...] = points[0:GAUSS]
+    weight[...] = jnp.zeros(weight.shape, F32)
+    weight[0:CELLS, 0:GAUSS] = potential[...]
+    flipped = jnp.concatenate([points[0:HALF].T, points[HALF:].T], axis=1)
+    high, low = split(points[...])
+    both = jnp.concatenate([high, low], axis=1)
+    for cell in range(CELLS):
+        rows = slice(cell * HALF, cell * HALF + HALF)
+        named = nodes[cell : cell + 1]
+        wanted = column(named)
+        for start in range(0, EXT, HALF):
+            pick[rows, start : start + HALF] = one_hot(wanted, lane + float(start))
+        place[:, rows] = one_hot(targets[...], named)
+        left_high, left_low = split(flipped * weight[cell : cell + 1])
+        product = joined(dot(left_high, both)) + dot(left_low, high)
+        matrix[rows] = product + scales[cell] * square[...]
+    masses[...] = jnp.ones(masses.shape, F32)
+    masses[0:1, 0:OWN] = mass[...]
+    halfwidth, _ = halfwidth_of(spectrum)
+    for at in range(0, OWN_PAD, HALF):
+        size = min(HALF, OWN_PAD - at)
+        own_scale[at : at + size] = 1.0 / (column(masses[0:1, at : at + HALF])[0:size] * halfwidth)
+
+
+def first_kernel(
+    spectrum, own, ghost, pick, place, matrix, own_out, ghost_out, bottom_out, scale_out, ext, cell
+):
     outs = (own_out, ghost_out, bottom_out)
     apply_cells(own[...], ghost[...], pick, place, matrix, ext, cell, outs)
+    halfwidth, _ = halfwidth_of(spectrum)
+    node = lax.broadcasted_iota(jnp.int32, (FACE_PAD, HALF), 0)
+    for at in range(0, FACE_PAD, HALF):
+        size = min(HALF, FACE_PAD - at)
+        mass_row = FACE + at // HALF
+        mass = column(ghost[mass_row : mass_row + 1])[0:size]
+        live = (mass > 0.0) & (node[at : at + size] < FACE)
+        scale = 1.0 / (jnp.where(live, mass, 1.0) * halfwidth)
+        scale_out[at : at + size] = jnp.where(live, scale, 0.0)
 
 
 def next_values(step, refs):
-    (beta, own_sum, ghost_sum, from_below, from_above, spread, own_scale, ghost_scale) = refs[:8]
+    (spectrum, own_sum, ghost_sum, from_below, from_above, spread, own_scale, ghost_scale) = refs[:8]
     factor = 1.0 if step == 0 else 2.0
     high, low = split(from_below[...])
-    arrived = dot(spread[...], high) + dot(spread[...], low)
+    arriving = jnp.concatenate([high, low], axis=1)
+    arriving = jnp.concatenate([arriving, jnp.zeros((2 * HALF - FACE_PAD, 2 * HALF), BF16)], axis=0)
+    arrived = joined(dot(spread[...], arriving))
     own = refs[8][...]
     ghost = refs[9][...]
-    shift = beta[0]
+    halfwidth, centre = halfwidth_of(spectrum)
+    shift = centre / halfwidth
     new_own = factor * (own_scale[...] * (own_sum[...] + arrived[0:OWN_PAD]) - shift * own)
     new_ghost = factor * (ghost_scale[...] * (ghost_sum[...] + from_above[...]) - shift * ghost)
     if step > 0:
@@ -209,7 +331,7 @@
 
 
 def call(kernel, shapes, scratch, operands, scalars=0):
-    out = [jax.ShapeDtypeStruct(shape, F32) for shape in shapes]
+    out = [jax.ShapeDtypeStruct(shape[:2], (shape + (F32,))[2]) for shape in shapes]
     in_vmem = pl.BlockSpec(memory_space=pltpu.VMEM)
     specs = [pl.BlockSpec(memory_space=pltpu.SMEM)] * scalars
     specs = specs + [in_vmem] * (len(operands) - scalars)
@@ -231,64 +353,63 @@
 def per_device(
     block, conn, bottom, cell_scale, potential, mass, stiffness, interp, occupancy, spectrum
 ):
-    dom = ("x", "zh", "zl", "y")
+    dom = DOM
     count = lax.axis_size(dom)
     down = [(i + 1, i) for i in range(count - 1)]
     up = [(i, i + 1) for i in range(count - 1)]
-    halfwidth = (spectrum[1] - spectrum[0]) / 2.0
-    centre = (spectrum[1] + spectrum[0]) / 2.0
-
-    own = jnp.pad(block.T, ((0, OWN_PAD - OWN), (0, 0)))
-    masses = jnp.pad(jnp.take(mass, bottom), (0, 2 * HALF - FACE)).reshape(2, HALF)
-    face = jnp.concatenate(
-        [jnp.take(own, bottom, axis=0), masses, jnp.zeros((FACE_PAD - FACE - 2, HALF), F32)], axis=0
+    listed = bottom.reshape(1, FACE)
+    mass_row = mass.reshape(1, OWN)
+    face, own, spread = call(
+        face_kernel,
+        [(FACE_PAD, HALF), (OWN_PAD, HALF), (GHOST_AT, 2 * HALF, BF16)],
+        [
+            pltpu.VMEM((8, 2 * HALF), F32),
+            pltpu.VMEM((8, GHOST_AT), F32),
+            pltpu.VMEM((FACE_PAD, GHOST_AT), BF16),
+            pltpu.VMEM((GHOST_AT, 2 * HALF), BF16),
+        ],
+        (block.T, listed, mass_row),
     )
     ghost = lax.ppermute(face, dom, down)
-    ghost_mass = ghost[FACE : FACE + 2].reshape(-1)[:FACE_PAD]
     own_mass = jnp.pad(mass, (0, OWN_PAD - OWN))
-
-    def inverse_mass(values, used):
-        live = (jnp.arange(values.shape[0]) < used) & (values > 0.0)
-        scale = jnp.where(live, 1.0 / (jnp.where(live, values, 1.0) * halfwidth), 0.0)
-        return jnp.broadcast_to(scale[:, None], (values.shape[0], HALF))
-
-    own_scale = inverse_mass(own_mass, OWN)
-    ghost_scale = inverse_mass(ghost_mass, FACE)
-
-    nodes = jnp.where(conn < OWN, conn, conn + (GHOST_AT - OWN))
-    nodes = jnp.pad(nodes.T, ((0, 0), (0, 128 - NPC)), constant_values=-1).reshape(PICK)
-    listed = jnp.pad(bottom, (0, FACE_PAD - FACE), constant_values=-2)
-    targets = jnp.concatenate(
+    *tables, own_scale, wide = call(
+        table_kernel,
         [
-            jnp.arange(OWN_PAD),
-            GHOST_AT + jnp.arange(FACE_PAD),
-            listed,
-            jnp.full((ROWS - OWN_PAD - 2 * FACE_PAD,), -2),
-        ]
-    )
-    pick = (nodes[:, None] == jnp.arange(EXT)[None, :]).astype(BF16)
-    place = (targets[:, None] == nodes[None, :]).astype(BF16)
-    spread = (jnp.arange(688)[:, None] == listed[None, :]).astype(BF16)
-
-    wide = jnp.pad(interp, ((0, 0), (0, 128 - NPC)))
-    weighted = (wide[:, None, :] * potential[:, :, None]).reshape(GAUSS, PICK)
-    cells = dot6(weighted, wide, ((0,), (0,)))
-    stiff = jnp.pad(stiffness, ((0, 128 - NPC), (0, 128 - NPC)))
-    cells = cells + (cell_scale[:, None, None] * stiff[None]).reshape(PICK, 128)
-    tables = (pick, place, cells)
+            (PICK, EXT, BF16),
+            (ROWS, PICK, BF16),
+            (PICK, HALF),
+            (OWN_PAD, HALF),
+            (GAUSS, HALF),
+        ],
+        [
+            pltpu.VMEM((16, HALF), F32),
+            pltpu.VMEM((8, 2 * HALF), F32),
+            pltpu.VMEM((ROWS, HALF), F32),
+            pltpu.VMEM((HALF, HALF), F32),
+            pltpu.VMEM((2 * HALF, HALF), F32),
+            pltpu.VMEM((16, 2 * HALF), F32),
+            pltpu.VMEM((8, GHOST_AT), F32),
+        ],
+        (spectrum, cell_scale, conn.T, listed, interp, potential.T, stiffness, mass_row),
+        2,
+    )
+    tables = tuple(tables)
 
     scratch = [pltpu.VMEM((EXT, 2 * HALF), BF16), pltpu.VMEM((PICK, 2 * HALF), BF16)]
     own_shape, face_shape = (OWN_PAD, HALF), (FACE_PAD, HALF)
-    sums = call(
-        first_kernel, [own_shape, face_shape, face_shape], scratch, (own, ghost) + tables
-    )
-    beta = (centre / halfwidth).reshape(1)
+    *sums, ghost_scale = call(
+        first_kernel,
+        [own_shape, face_shape, face_shape, face_shape],
+        scratch,
+        (spectrum, own, ghost) + tables,
+        1,
+    )
     last = ()
     for step in range(DEG):
         own_sum, ghost_sum, bottom_sum = sums
         from_above = lax.ppermute(bottom_sum, dom, down)
         from_below = lax.ppermute(ghost_sum, dom, up)
-        operands = (beta, own_sum, ghost_sum, from_below, from_above, spread, own_scale)
+        operands = (spectrum, own_sum, ghost_sum, from_below, from_above, spread, own_scale)
         operands = operands + (ghost_scale, own, ghost) + last
         last = (own, ghost)
         if step < DEG - 1:
@@ -312,11 +433,13 @@
     term = jnp.concatenate(
         [dot6(whole[half, :OWN_PAD], weighted, ((0,), (0,))) for half in range(2)], axis=0
     )
-    near, far = ("zl", "y"), ("x", "zh")
+    near = ("xl", "zl", "yl")
     size = lax.axis_size(near)
     term = term * (1.0 / (count * OWN))
     pieces = lax.all_to_all(term.reshape(size, ORBS // size, HALF), near, 0, 0)
-    piece = jnp.sum(gather_all(jnp.sum(pieces, axis=0), far), axis=0)
+    piece = jnp.sum(pieces, axis=0)
+    for far in (("xh", "zm"), ("zh", "yh")):
+        piece = jnp.sum(gather_all(piece, far), axis=0)
     gram = lax.all_gather(gather_all(piece, near).reshape(ORBS, HALF), "orb", axis=0)
 
     (density,) = call(
@@ -328,16 +451,18 @@
             pltpu.VMEM((EXT, 4 * HALF), BF16),
             pltpu.VMEM((CELLS, GAUSS, ORBS), F32),
         ],
-        (gram, whole, pick, wide),
+        (gram, whole, tables[0], wide),
     )
     return density
 
 
 def solution(mesh):
     side = round(mesh.shape["dom"] ** (1.0 / 3.0))
-    shape = (side, side // 2, 2, side, 2)
-    torus = Mesh(mesh.devices.reshape(shape), ("x", "zh", "zl", "y", "orb"))
-    dom = ("x", "zh", "zl", "y")
+    half = side // 2
+    quarter = max(1, half // 2)
+    shape = (half, 2, quarter, half // quarter, 2, half, 2, 2)
+    torus = Mesh(mesh.devices.reshape(shape), DOM + ("orb",))
+    dom = DOM
     in_specs = (
         P("orb", dom),
         P(None, dom),

time: 164 us -> 172 us (1.049)
  waiting for transfers between devices: 4.58 us -> 13.5 us
  other arithmetic: 7.64 us -> 2.77 us
  Pallas kernels: 30.6 us -> 35.3 us
  blocking collectives: 89.2 us -> 92.6 us
  between operations: 3.14 us -> 0.21 us
  local copies, waits for them, and re-layouts: 5.81 us -> 7.54 us
    ppermute x3, waiting for transfers between devices: 0.36 us -> 12.7 us  [per_device(): from_above = lax.ppermute(bottom_sum, dom, down)]
    all_to_all x1, blocking collectives: 17.5 us -> 24.3 us  [per_device(): pieces = lax.all_to_all(term.reshape(size, ORBS // size, HALF), near, 0, 0)]
    unnamed x22, local copies, waits for them, and re-layouts: 0.58 us -> 6.13 us
    all_gather x1, blocking collectives: 19 us -> 13.8 us  [per_device(): whole = lax.all_gather(field, 'orb', axis=0)]
    pallas_call x5 -> x7, Pallas kernels: 30.6 us -> 35.3 us  [call(): pl.pallas_call(kernel, out_shape=out, in_specs=specs, out_specs=[in_vmem]...]
    ppermute x3, waiting for transfers between devices: 4.22 us -> 0.78 us  [per_device(): from_below = lax.ppermute(ghost_sum, dom, up)]
    gather x2 -> x0, local copies, waits for them, and re-layouts: 2.6 us -> none  [the longest x1 1.92 us: per_device(): jnp.take(mass, bottom)]
    convert_element_type x3 -> x0, other arithmetic: 2.47 us -> none  [the longest x1 1.91 us: per_device(): place = (targets[:, None] == nodes[None, :]).astype(BF16)]
  transfers between devices with their start and end apart: 7 -> 7, of which waited for: 4 -> 6; matrix products, arithmetic and copies ran while one was open for 4% -> 0% of each run, Pallas kernels for 0% -> 1%
where the time goes in v3:
time: 172 us
  blocking collectives  92.6 us (54%)
  Pallas kernels  35.3 us (21%)
  starting transfers between devices  17.9 us (10%)
  waiting for transfers between devices  13.5 us (8%)
  local copies, waits for them, and re-layouts  7.54 us (4%)
  other arithmetic  2.77 us (2%)
  matrix products  1.82 us (1%)
    all_to_all x3, blocking collectives, gather_all(): lax.all_to_all(jnp.broadcast_to(value[None], (count,) + value.shape), axe...  47.1 us
    pallas_call x7, Pallas kernels, call(): pl.pallas_call(kernel, out_shape=out, in_specs=specs, out_specs=[in_vmem]...  35.3 us
    all_to_all x1, blocking collectives, per_device(): pieces = lax.all_to_all(term.reshape(size, ORBS // size, HALF), near, 0, 0)  24.3 us
    all_gather x1, blocking collectives, per_device(): whole = lax.all_gather(field, 'orb', axis=0)  13.8 us
    ppermute x3, starting transfers between devices, per_device(): from_below = lax.ppermute(ghost_sum, dom, up)  12.7 us
    ppermute x3, waiting for transfers between devices, per_device(): from_above = lax.ppermute(bottom_sum, dom, down)  12.7 us
    all_gather x1, blocking collectives, per_device(): lax.all_gather(gather_all(piece, near).reshape(ORBS, HALF), 'orb', axis=0)  7.38 us
    unnamed x22, local copies, waits for them, and re-layouts  6.13 us
  transfers between devices with their start and end apart: 7, of which 6 were waited for; matrix products, arithmetic and copies ran while one was open for 0% of the time, Pallas kernels for 1%

profile of v3, /device:TPU:1, one launch (start us, length us, event | category | flops | bytes accessed | tf_op | source)
XLA Modules:
  0.0 171.6 jit_solution(17206918389082637204)
XLA Ops:
  0.7 1.0 copy-done
  2.8 1.3 collective-permute-start
  8.6 2.5 %shard_map.101 = (bf16[1152,1024]{1,0:T(8,128)(2,1)S(1)}, bf16[1040,1152]{1,0:T(8,128)(2,1)S(1)}, f32[1152,128]{1,0:T(8,128)S(1)}, f32[680,128]{1,0:T(8,128)S(1)}, f32[216,128]{1,0:T(8,128)S(1)}) custom-call(f32[2]{0:T(128)S(1)} %copy-done.4, f32[9]{0:T(128)S(1)} %copy-done.8, s32[9,125]{1,0:T(8,128)S(1)} %bitcast.19, s32[1,169]{1,0:T(1,128)S(1)} %bitcast.21, ...), custom_call_target="tpu_custom_call" | custom-call | tf_op jit(solution)/shard_map/pallas_call | solution.py:338
  11.1 3.4 %shard_map.102 = (f32[680,128]{1,0:T(8,128)S(1)}, f32[176,128]{1,0:T(8,128)S(1)}, f32[176,128]{1,0:T(8,128)S(1)}, f32[176,128]{1,0:T(8,128)S(1)}) custom-call(f32[2]{0:T(128)S(1)} %copy-done.4, f32[680,128]{1,0:T(8,128)S(1)} %get-tuple-element.27.own.refs_8_.refs_10_, f32[176,128]{1,0:T(8,128)S(1)} %collective-permute-done.ghost.refs_9_.refs_11_, ...), custom_call_target="tpu_custom_call" | custom-call | tf_op jit(solution)/shard_map/pallas_call | solution.py:338
  14.6 4.8 %collective-permute-start.1 = (f32[176,128]{1,0:T(8,128)S(1)}, f32[176,128]{1,0:T(8,128)S(1)}, u32[]{:S(2)}, u32[]{:S(2)}) collective-permute-start(f32[176,128]{1,0:T(8,128)S(1)} %get-tuple-element.33.refs_2_), channel_id=1, source_target_pairs={{0,2},{2,4},{4,6},{6,8},{8,10},{10,12},{12,14},{14,16},{16,18},{18... | collective-permute-start | bytes 270344 | tf_op jit(solution)/shard_map/ppermute | solution.py:411
  19.3 1.3 collective-permute-start.2
  20.9 3.7 %collective-permute-done.2.refs_4_ = f32[176,128]{1,0:T(8,128)S(1)} collective-permute-done((f32[176,128]{1,0:T(8,128)S(1)}, f32[176,128]{1,0:T(8,128)S(1)}, u32[]{:S(2)}, u32[]{:S(2)}) %collective-permute-start.2) | collective-permute-done | bytes 90144 | tf_op jit(solution)/shard_map/ppermute | solution.py:410
  24.6 3.6 %shard_map.103 = (f32[680,128]{1,0:T(8,128)S(1)}, f32[176,128]{1,0:T(8,128)S(1)}, f32[680,128]{1,0:T(8,128)S(1)}, f32[176,128]{1,0:T(8,128)S(1)}, f32[176,128]{1,0:T(8,128)S(1)}) custom-call(f32[2]{0:T(128)S(1)} %copy-done.5, f32[680,128]{1,0:T(8,128)S(1)} %get-tuple-element.32.refs_1_, f32[176,128]{1,0:T(8,128)S(1)} %get-tuple-element.33.refs_2_, ...), custom_call_target="tpu_custom_call" | custom-call | tf_op jit(solution)/shard_map/pallas_call | solution.py:338
  28.2 3.4 %collective-permute-start.3 = (f32[176,128]{1,0:T(8,128)S(1)}, f32[176,128]{1,0:T(8,128)S(1)}, u32[]{:S(2)}, u32[]{:S(2)}) collective-permute-start(f32[176,128]{1,0:T(8,128)S(1)} %get-tuple-element.39.refs_2_), channel_id=1, source_target_pairs={{0,2},{2,4},{4,6},{6,8},{8,10},{10,12},{12,14},{14,16},{16,18},{18... | collective-permute-start | bytes 270344 | tf_op jit(solution)/shard_map/ppermute | solution.py:411
  31.6 1.3 collective-permute-start.4
  33.2 4.9 %collective-permute-done.4.refs_4_ = f32[176,128]{1,0:T(8,128)S(1)} collective-permute-done((f32[176,128]{1,0:T(8,128)S(1)}, f32[176,128]{1,0:T(8,128)S(1)}, u32[]{:S(2)}, u32[]{:S(2)}) %collective-permute-start.4) | collective-permute-done | bytes 90144 | tf_op jit(solution)/shard_map/ppermute | solution.py:410
  38.0 3.6 %shard_map.104 = (f32[680,128]{1,0:T(8,128)S(1)}, f32[176,128]{1,0:T(8,128)S(1)}, f32[680,128]{1,0:T(8,128)S(1)}, f32[176,128]{1,0:T(8,128)S(1)}, f32[176,128]{1,0:T(8,128)S(1)}) custom-call(f32[2]{0:T(128)S(1)} %copy-done.5, f32[680,128]{1,0:T(8,128)S(1)} %get-tuple-element.38.refs_1_, f32[176,128]{1,0:T(8,128)S(1)} %get-tuple-element.39.refs_2_, ...), custom_call_target="tpu_custom_call" | custom-call | tf_op jit(solution)/shard_map/pallas_call | solution.py:338
  41.7 4.6 %collective-permute-start.5 = (f32[176,128]{1,0:T(8,128)S(1)}, f32[176,128]{1,0:T(8,128)S(1)}, u32[]{:S(2)}, u32[]{:S(2)}) collective-permute-start(f32[176,128]{1,0:T(8,128)S(1)} %get-tuple-element.44.refs_2_), channel_id=1, source_target_pairs={{0,2},{2,4},{4,6},{6,8},{8,10},{10,12},{12,14},{14,16},{16,18},{18... | collective-permute-start | bytes 270344 | tf_op jit(solution)/shard_map/ppermute | solution.py:411
  46.2 1.3 collective-permute-start.6
  47.8 4.1 %collective-permute-done.6.refs_4_ = f32[176,128]{1,0:T(8,128)S(1)} collective-permute-done((f32[176,128]{1,0:T(8,128)S(1)}, f32[176,128]{1,0:T(8,128)S(1)}, u32[]{:S(2)}, u32[]{:S(2)}) %collective-permute-start.6) | collective-permute-done | bytes 90144 | tf_op jit(solution)/shard_map/ppermute | solution.py:410
  52.8 13.8 %all-gather = f32[1728,128]{1,0:T(8,128)S(1)} all-gather(f32[864,128]{1,0:T(8,128)S(1)} %shard_map.105), channel_id=2, replica_groups=mesh['xh'=4,'xl'=2,'zh'=2,'zm'=2,'zl'=2,'yh'=4,'yl'=2,'orb'=2] {'orb'}, dimensions={0}, use_global_device_ids=true | all-gather | bytes 1327104 | tf_op jit(solution)/shard_map/all_gather | solution.py:430
  68.5 24.3 %all_to_all.20 = f32[8,32,128]{2,1,0:T(8,128)} all-to-all(f32[8,32,128]{2,1,0:T(8,128)S(1)} %bitcast.24), channel_id=1, replica_groups=mesh['xh'=4,'xl'=2,'zh'=2,'zm'=2,'zl'=2,'yh'=4,'yl'=2,'orb'=2] {'xl','zl..., dimensions={0} | all-to-all | bytes 262144 | tf_op jit(solution)/shard_map/all_to_all | solution.py:439
  92.7 0.9 reduce_sum.27
  93.7 19.2 %all_to_all.21 = f32[8,32,128]{2,1,0:T(8,128)} all-to-all(f32[8,32,128]{2,1,0:T(8,128)S(1)} %broadcast_in_dim.6), channel_id=1, replica_groups=mesh['xh'=4,'xl'=2,'zh'=2,'zm'=2,'zl'=2,'yh'=4,'yl'=2,'orb'=2] {'xh','zm'}, dimensions={0} | all-to-all | bytes 262144 | tf_op jit(solution)/shard_map/all_to_all | solution.py:350
  112.9 0.9 reduce_sum.28
  113.8 20.6 %all_to_all.22 = f32[8,32,128]{2,1,0:T(8,128)} all-to-all(f32[8,32,128]{2,1,0:T(8,128)S(1)} %broadcast_in_dim.7), channel_id=1, replica_groups=mesh['xh'=4,'xl'=2,'zh'=2,'zm'=2,'zl'=2,'yh'=4,'yl'=2,'orb'=2] {'zh','yh'}, dimensions={0} | all-to-all | bytes 262144 | tf_op jit(solution)/shard_map/all_to_all | solution.py:350
  135.4 7.3 %all_to_all.23 = f32[8,32,128]{2,1,0:T(8,128)S(1)} all-to-all(f32[8,32,128]{2,1,0:T(8,128)S(1)} %broadcast_in_dim.8), channel_id=1, replica_groups=mesh['xh'=4,'xl'=2,'zh'=2,'zm'=2,'zl'=2,'yh'=4,'yl'=2,'orb'=2] {'xl','zl..., dimensions={0} | all-to-all | bytes 262144 | tf_op jit(solution)/shard_map/all_to_all | solution.py:350
  142.7 7.4 %all_gather.11.gram = f32[2,256,128]{2,1,0:T(8,128)S(1)} all-gather(f32[1,256,128]{2,1,0:T(8,128)S(1)} %bitcast.23), channel_id=1, replica_groups=mesh['xh'=4,'xl'=2,'zh'=2,'zm'=2,'zl'=2,'yh'=4,'yl'=2,'orb'=2] {'orb'}, dimensions={0}, use_global_device_ids=true | all-gather | bytes 393216 | tf_op jit(solution)/shard_map/all_gather | solution.py:443
  150.1 20.8 %shard_map.106 = f32[216,9]{1,0:T(8,128)S(1)} custom-call(f32[2,256,128]{2,1,0:T(8,128)S(1)} %all_gather.11.gram, f32[2,864,128]{2,1,0:T(8,128)S(1)} %bitcast.16, bf16[1152,1024]{1,0:T(8,128)(2,1)S(1)} %get-tuple-element.29.pick.refs_10_.refs_12_, f32[216,128]{1,0:T(8,128)S(1)} %get-tuple-element.48.interp), custom_call_target="tpu_custom_call" | custom-call | tf_op jit(solution)/shard_map/pallas_call | solution.py:338
  (37 shorter events, 11.4 us)
Async XLA Ops:
  0.7 1.0 copy-start
  1.7 0.7 copy-start.7
  2.8 8.3 %collective-permute-start = (f32[176,128]{1,0:T(8,128)S(1)}, f32[176,128]{1,0:T(8,128)S(1)}, u32[]{:S(2)}, u32[]{:S(2)}) collective-permute-start(f32[176,128]{1,0:T(8,128)S(1)} %get-tuple-element.28), channel_id=1, source_target_pairs={{2,0},{4,2},{6,4},{8,6},{10,8},{12,10},{14,12},{16,14},{18,16},{20... | collective-permute-start | bytes 270344 | tf_op jit(solution)/shard_map/ppermute | solution.py:373
  4.1 0.9 copy-start.1
  5.0 0.8 copy-start.2
  5.9 0.7 copy-start.3
  6.6 0.7 copy-start.4
  7.2 0.7 copy-start.6
  7.9 0.7 copy-start.8
  11.1 13.5 %copy-start.5 = (f32[2]{0:T(128)S(1)}, f32[2]{0:T(128)}, u32[]{:S(2)}) copy-start(f32[2]{0:T(128)} %refs_0_.5) | copy-start | bytes 28
  14.6 6.3 %collective-permute-start.1 = (f32[176,128]{1,0:T(8,128)S(1)}, f32[176,128]{1,0:T(8,128)S(1)}, u32[]{:S(2)}, u32[]{:S(2)}) collective-permute-start(f32[176,128]{1,0:T(8,128)S(1)} %get-tuple-element.33.refs_2_), channel_id=1, source_target_pairs={{0,2},{2,4},{4,6},{6,8},{8,10},{10,12},{12,14},{14,16},{16,18},{18... | collective-permute-start | bytes 270344 | tf_op jit(solution)/shard_map/ppermute | solution.py:411
  19.3 5.3 %collective-permute-start.2 = (f32[176,128]{1,0:T(8,128)S(1)}, f32[176,128]{1,0:T(8,128)S(1)}, u32[]{:S(2)}, u32[]{:S(2)}) collective-permute-start(f32[176,128]{1,0:T(8,128)S(1)} %get-tuple-element.34), channel_id=1, source_target_pairs={{2,0},{4,2},{6,4},{8,6},{10,8},{12,10},{14,12},{16,14},{18,16},{20... | collective-permute-start | bytes 270344 | tf_op jit(solution)/shard_map/ppermute | solution.py:410
  28.2 4.9 %collective-permute-start.3 = (f32[176,128]{1,0:T(8,128)S(1)}, f32[176,128]{1,0:T(8,128)S(1)}, u32[]{:S(2)}, u32[]{:S(2)}) collective-permute-start(f32[176,128]{1,0:T(8,128)S(1)} %get-tuple-element.39.refs_2_), channel_id=1, source_target_pairs={{0,2},{2,4},{4,6},{6,8},{8,10},{10,12},{12,14},{14,16},{16,18},{18... | collective-permute-start | bytes 270344 | tf_op jit(solution)/shard_map/ppermute | solution.py:411
  31.6 6.4 %collective-permute-start.4 = (f32[176,128]{1,0:T(8,128)S(1)}, f32[176,128]{1,0:T(8,128)S(1)}, u32[]{:S(2)}, u32[]{:S(2)}) collective-permute-start(f32[176,128]{1,0:T(8,128)S(1)} %get-tuple-element.40), channel_id=1, source_target_pairs={{2,0},{4,2},{6,4},{8,6},{10,8},{12,10},{14,12},{16,14},{18,16},{20... | collective-permute-start | bytes 270344 | tf_op jit(solution)/shard_map/ppermute | solution.py:410
  38.0 9.5 %copy-start.10 = (f32[676]{0:T(1024)S(1)}, f32[676]{0:T(1024)}, u32[]{:S(2)}) copy-start(f32[676]{0:T(1024)} %param.15) | copy-start | bytes 8116
  38.0 13.9 %copy-start.9 = (f32[128]{0:T(128)S(1)}, f32[128]{0:T(128)}, u32[]{:S(2)}) copy-start(f32[128]{0:T(128)} %param.18) | copy-start | bytes 1540
  41.7 6.2 %collective-permute-start.5 = (f32[176,128]{1,0:T(8,128)S(1)}, f32[176,128]{1,0:T(8,128)S(1)}, u32[]{:S(2)}, u32[]{:S(2)}) collective-permute-start(f32[176,128]{1,0:T(8,128)S(1)} %get-tuple-element.44.refs_2_), channel_id=1, source_target_pairs={{0,2},{2,4},{4,6},{6,8},{8,10},{10,12},{12,14},{14,16},{16,18},{18... | collective-permute-start | bytes 270344 | tf_op jit(solution)/shard_map/ppermute | solution.py:411
  46.2 5.7 %collective-permute-start.6 = (f32[176,128]{1,0:T(8,128)S(1)}, f32[176,128]{1,0:T(8,128)S(1)}, u32[]{:S(2)}, u32[]{:S(2)}) collective-permute-start(f32[176,128]{1,0:T(8,128)S(1)} %get-tuple-element.45), channel_id=1, source_target_pairs={{2,0},{4,2},{6,4},{8,6},{10,8},{12,10},{14,12},{16,14},{18,16},{20... | collective-permute-start | bytes 270344 | tf_op jit(solution)/shard_map/ppermute | solution.py:410

commit v4 on v3

--- a/solution.py
+++ b/solution.py
@@ -24,7 +24,7 @@
 ROWS = 1040
 OCC_AT = OWN_PAD + FACE_PAD
 FIELD = 864
-DOM = ("xh", "xl", "zh", "zm", "zl", "yh", "yl")
+DOM = ("x", "zh", "zl", "y")
 VMEM = 24 * 1024 * 1024
 F32 = jnp.float32
 BF16 = jnp.bfloat16
@@ -88,7 +88,20 @@
     return jnp.where(left == right, 1.0, 0.0).astype(BF16)
 
 
-def face_kernel(block, bottom, mass, face, own, spread, listed, terms, select, ext):
+def fetch(sources, targets, done):
+    copies = [
+        pltpu.make_async_copy(source, target, done.at[i])
+        for i, (source, target) in enumerate(zip(sources, targets, strict=True))
+    ]
+    for copy in copies:
+        copy.start()
+    for copy in copies:
+        copy.wait()
+
+
+def face_kernel(*refs):
+    face, own, spread, listed, terms, select, ext, block, bottom, mass, done = refs[3:]
+    fetch(refs[:3], (block, bottom, mass), done)
     own[0:OWN] = block[...]
     own[OWN:OWN_PAD] = jnp.zeros((OWN_PAD - OWN, HALF), F32)
     ext[OWN_PAD:GHOST_AT] = jnp.zeros((GHOST_AT - OWN_PAD, 2 * HALF), BF16)
@@ -123,28 +136,12 @@
     return (high - low) * 0.5, (high + low) * 0.5
 
 
-def table_kernel(
-    spectrum,
-    scales,
-    conn,
-    bottom,
-    interp,
-    potential,
-    stiffness,
-    mass,
-    pick,
-    place,
-    matrix,
-    own_scale,
-    wide,
-    nodes,
-    listed,
-    targets,
-    square,
-    points,
-    weight,
-    masses,
-):
+def table_kernel(*refs):
+    pick, place, matrix, own_scale, wide, scalars = refs[8:14]
+    nodes, listed, targets, square, points, weight, masses = refs[14:21]
+    scales, spectrum, conn, bottom, interp, potential, stiffness, mass, done = refs[21:]
+    targets_of = (spectrum, scales, conn, bottom, interp, potential, stiffness, mass)
+    fetch(refs[:8], targets_of, done)
     nodes[...] = jnp.full(nodes.shape, -1.0, F32)
     own_node = conn[...] < OWN
     named = jnp.where(own_node, conn[...], conn[...] + (GHOST_AT - OWN))
@@ -181,18 +178,21 @@
         matrix[rows] = product + scales[cell] * square[...]
     masses[...] = jnp.ones(masses.shape, F32)
     masses[0:1, 0:OWN] = mass[...]
-    halfwidth, _ = halfwidth_of(spectrum)
+    halfwidth, centre = halfwidth_of(spectrum)
+    scalars[...] = jnp.zeros(scalars.shape, F32)
+    scalars[0:1] = halfwidth
+    scalars[1:2] = centre / halfwidth
     for at in range(0, OWN_PAD, HALF):
         size = min(HALF, OWN_PAD - at)
         own_scale[at : at + size] = 1.0 / (column(masses[0:1, at : at + HALF])[0:size] * halfwidth)
 
 
 def first_kernel(
-    spectrum, own, ghost, pick, place, matrix, own_out, ghost_out, bottom_out, scale_out, ext, cell
+    scalars, own, ghost, pick, place, matrix, own_out, ghost_out, bottom_out, scale_out, ext, cell
 ):
     outs = (own_out, ghost_out, bottom_out)
     apply_cells(own[...], ghost[...], pick, place, matrix, ext, cell, outs)
-    halfwidth, _ = halfwidth_of(spectrum)
+    halfwidth = scalars[0:1]
     node = lax.broadcasted_iota(jnp.int32, (FACE_PAD, HALF), 0)
     for at in range(0, FACE_PAD, HALF):
         size = min(HALF, FACE_PAD - at)
@@ -204,7 +204,7 @@
 
 
 def next_values(step, refs):
-    (spectrum, own_sum, ghost_sum, from_below, from_above, spread, own_scale, ghost_scale) = refs[:8]
+    (scalars, own_sum, ghost_sum, from_below, from_above, spread, own_scale, ghost_scale) = refs[:8]
     factor = 1.0 if step == 0 else 2.0
     high, low = split(from_below[...])
     arriving = jnp.concatenate([high, low], axis=1)
@@ -212,8 +212,7 @@
     arrived = joined(dot(spread[...], arriving))
     own = refs[8][...]
     ghost = refs[9][...]
-    halfwidth, centre = halfwidth_of(spectrum)
-    shift = centre / halfwidth
+    shift = scalars[1:2]
     new_own = factor * (own_scale[...] * (own_sum[...] + arrived[0:OWN_PAD]) - shift * own)
     new_ghost = factor * (ghost_scale[...] * (ghost_sum[...] + from_above[...]) - shift * ghost)
     if step > 0:
@@ -330,11 +329,13 @@
         out[:, cell : cell + 1] = jnp.sum(value * value * weights, axis=1, keepdims=True)
 
 
-def call(kernel, shapes, scratch, operands, scalars=0):
+def call(kernel, shapes, scratch, operands, far=0):
     out = [jax.ShapeDtypeStruct(shape[:2], (shape + (F32,))[2]) for shape in shapes]
     in_vmem = pl.BlockSpec(memory_space=pltpu.VMEM)
-    specs = [pl.BlockSpec(memory_space=pltpu.SMEM)] * scalars
-    specs = specs + [in_vmem] * (len(operands) - scalars)
+    specs = [pl.BlockSpec(memory_space=pltpu.HBM)] * far + [in_vmem] * (len(operands) - far)
+    operands = list(operands)
+    for i in range(far):
+        operands[i] = pltpu.with_memory_space_constraint(operands[i], pltpu.HBM)
     return pl.pallas_call(
         kernel,
         out_shape=out,
@@ -367,12 +368,17 @@
             pltpu.VMEM((8, GHOST_AT), F32),
             pltpu.VMEM((FACE_PAD, GHOST_AT), BF16),
             pltpu.VMEM((GHOST_AT, 2 * HALF), BF16),
+            pltpu.VMEM((OWN, HALF), F32),
+            pltpu.VMEM((1, FACE), jnp.int32),
+            pltpu.VMEM((1, OWN), F32),
+            pltpu.SemaphoreType.DMA((3,)),
         ],
         (block.T, listed, mass_row),
+        3,
     )
     ghost = lax.ppermute(face, dom, down)
     own_mass = jnp.pad(mass, (0, OWN_PAD - OWN))
-    *tables, own_scale, wide = call(
+    *tables, own_scale, wide, scalars = call(
         table_kernel,
         [
             (PICK, EXT, BF16),
@@ -380,6 +386,7 @@
             (PICK, HALF),
             (OWN_PAD, HALF),
             (GAUSS, HALF),
+            (8, HALF),
         ],
         [
             pltpu.VMEM((16, HALF), F32),
@@ -389,9 +396,18 @@
             pltpu.VMEM((2 * HALF, HALF), F32),
             pltpu.VMEM((16, 2 * HALF), F32),
             pltpu.VMEM((8, GHOST_AT), F32),
+            pltpu.SMEM((CELLS,), F32),
+            pltpu.SMEM((2,), F32),
+            pltpu.VMEM((CELLS, NPC), jnp.int32),
+            pltpu.VMEM((1, FACE), jnp.int32),
+            pltpu.VMEM((GAUSS, NPC), F32),
+            pltpu.VMEM((CELLS, GAUSS), F32),
+            pltpu.VMEM((NPC, NPC), F32),
+            pltpu.VMEM((1, OWN), F32),
+            pltpu.SemaphoreType.DMA((8,)),
         ],
         (spectrum, cell_scale, conn.T, listed, interp, potential.T, stiffness, mass_row),
-        2,
+        8,
     )
     tables = tuple(tables)
 
@@ -401,15 +417,14 @@
         first_kernel,
         [own_shape, face_shape, face_shape, face_shape],
         scratch,
-        (spectrum, own, ghost) + tables,
-        1,
+        (scalars, own, ghost) + tables,
     )
     last = ()
     for step in range(DEG):
         own_sum, ghost_sum, bottom_sum = sums
         from_above = lax.ppermute(bottom_sum, dom, down)
         from_below = lax.ppermute(ghost_sum, dom, up)
-        operands = (spectrum, own_sum, ghost_sum, from_below, from_above, spread, own_scale)
+        operands = (scalars, own_sum, ghost_sum, from_below, from_above, spread, own_scale)
         operands = operands + (ghost_scale, own, ghost) + last
         last = (own, ghost)
         if step < DEG - 1:
@@ -418,14 +433,12 @@
                 [own_shape, face_shape, own_shape, face_shape, face_shape],
                 scratch,
                 operands + tables,
-                1,
             )
     (field,) = call(
         functools.partial(last_kernel, DEG - 1),
         [(FIELD, HALF)],
         [],
         operands + (occupancy.reshape(1, HALF),),
-        1,
     )
     whole = lax.all_gather(field, "orb", axis=0)
 
@@ -433,13 +446,11 @@
     term = jnp.concatenate(
         [dot6(whole[half, :OWN_PAD], weighted, ((0,), (0,))) for half in range(2)], axis=0
     )
-    near = ("xl", "zl", "yl")
+    near, far = ("zl", "y"), ("x", "zh")
     size = lax.axis_size(near)
     term = term * (1.0 / (count * OWN))
     pieces = lax.all_to_all(term.reshape(size, ORBS // size, HALF), near, 0, 0)
-    piece = jnp.sum(pieces, axis=0)
-    for far in (("xh", "zm"), ("zh", "yh")):
-        piece = jnp.sum(gather_all(piece, far), axis=0)
+    piece = jnp.sum(gather_all(jnp.sum(pieces, axis=0), far), axis=0)
     gram = lax.all_gather(gather_all(piece, near).reshape(ORBS, HALF), "orb", axis=0)
 
     (density,) = call(
@@ -458,9 +469,7 @@
 
 def solution(mesh):
     side = round(mesh.shape["dom"] ** (1.0 / 3.0))
-    half = side // 2
-    quarter = max(1, half // 2)
-    shape = (half, 2, quarter, half // quarter, 2, half, 2, 2)
+    shape = (side, side // 2, 2, side, 2)
     torus = Mesh(mesh.devices.reshape(shape), DOM + ("orb",))
     dom = DOM
     in_specs = (

time: 172 us -> 158 us (0.919)
  blocking collectives: 92.6 us -> 84.6 us
  local copies, waits for them, and re-layouts: 7.54 us -> 2 us
    all_to_all x1, blocking collectives: 24.3 us -> 11 us  [per_device(): pieces = lax.all_to_all(term.reshape(size, ORBS // size, HALF), near, 0, 0)]
    all_to_all x3 -> x2, blocking collectives: 47.1 us -> 53.7 us  [gather_all(): lax.all_to_all(jnp.broadcast_to(value[None], (count,) + value.shape), axe...]
    unnamed x22 -> x4, local copies, waits for them, and re-layouts: 6.13 us -> 0.01 us
    ppermute x1, waiting for transfers between devices: 0.01 us -> 1.78 us  [per_device(): ghost = lax.ppermute(face, dom, down)]
  transfers between devices with their start and end apart: 7 -> 7, of which waited for: 6 -> 7; matrix products, arithmetic and copies ran while one was open for 0% -> 0% of each run, Pallas kernels for 1% -> 2%
where the time goes in v4:
time: 158 us; the launch traced here: 157 us
  blocking collectives  84.6 us (54%)
  Pallas kernels  34.6 us (22%)
  starting transfers between devices  17.5 us (11%)
  waiting for transfers between devices  14.3 us (9%)
  local copies, waits for them, and re-layouts  2 us (1%)
  other arithmetic  1.93 us (1%)
  matrix products  1.82 us (1%)
    all_to_all x2, blocking collectives, gather_all(): lax.all_to_all(jnp.broadcast_to(value[None], (count,) + value.shape), axe...  53.7 us
    pallas_call x7, Pallas kernels, call(): pl.pallas_call(kernel, out_shape=out, in_specs=specs, out_specs=[in_vmem]...  34.6 us
    all_gather x1, blocking collectives, per_device(): whole = lax.all_gather(field, 'orb', axis=0)  13.4 us
    ppermute x3, starting transfers between devices, per_device(): from_below = lax.ppermute(ghost_sum, dom, up)  12.4 us
    ppermute x3, waiting for transfers between devices, per_device(): from_above = lax.ppermute(bottom_sum, dom, down)  11.6 us
    all_to_all x1, blocking collectives, per_device(): pieces = lax.all_to_all(term.reshape(size, ORBS // size, HALF), near, 0, 0)  11 us
    all_gather x1, blocking collectives, per_device(): lax.all_gather(gather_all(piece, near).reshape(ORBS, HALF), 'orb', axis=0)  6.46 us
    ppermute x3, starting transfers between devices, per_device(): from_above = lax.ppermute(bottom_sum, dom, down)  3.88 us
  transfers between devices with their start and end apart: 7, of which 7 were waited for; matrix products, arithmetic and copies ran while one was open for 0% of the time, Pallas kernels for 2%

profile of v4, /device:TPU:1, one launch (start us, length us, event | category | flops | bytes accessed | tf_op | source)
XLA Modules:
  0.0 157.0 jit_solution(18379411709487315686)
XLA Ops:
  0.0 1.3 reshape.17.refs_7_.refs_2_
  1.3 1.5 shard_map.101
  2.8 1.3 collective-permute-start
  4.1 3.0 %shard_map.100 = (bf16[1152,1024]{1,0:T(8,128)(2,1)S(1)}, bf16[1040,1152]{1,0:T(8,128)(2,1)S(1)}, f32[1152,128]{1,0:T(8,128)S(1)}, f32[680,128]{1,0:T(8,128)S(1)...) custom-call(f32[2]{0:T(128)} %refs_0_.1, f32[9]{0:T(128)} %refs_1_.1, s32[9,125]{1,0:T(8,128)} %bitcast.22, ...), custom_call_target="tpu_custom_call" | custom-call | tf_op jit(solution)/shard_map/pallas_call | solution.py:339
  7.0 1.8 %collective-permute-done.ghost.refs_9_.refs_11_ = f32[176,128]{1,0:T(8,128)S(1)} collective-permute-done((f32[176,128]{1,0:T(8,128)S(1)}, f32[176,128]{1,0:T(8,128)S(1)}, u32[]{:S(2)}, u32[]{:S(2)}) %collective-permute-start) | collective-permute-done | bytes 90144 | tf_op jit(solution)/shard_map/ppermute | solution.py:379
  8.8 2.9 %shard_map.102 = (f32[680,128]{1,0:T(8,128)S(1)}, f32[176,128]{1,0:T(8,128)S(1)}, f32[176,128]{1,0:T(8,128)S(1)}, f32[176,128]{1,0:T(8,128)S(1)}) custom-call(f32[8,128]{1,0:T(8,128)S(1)} %get-tuple-element.28.scalars.refs_0_, f32[680,128]{1,0:T(8,128)S(1)} %get-tuple-element.29.own.refs_8_.refs_10_, ...), custom_call_target="tpu_custom_call" | custom-call | tf_op jit(solution)/shard_map/pallas_call | solution.py:339
  11.7 3.4 %collective-permute-start.1 = (f32[176,128]{1,0:T(8,128)S(1)}, f32[176,128]{1,0:T(8,128)S(1)}, u32[]{:S(2)}, u32[]{:S(2)}) collective-permute-start(f32[176,128]{1,0:T(8,128)S(1)} %get-tuple-element.35.refs_2_), channel_id=1, source_target_pairs={{0,2},{2,4},{4,6},{6,8},{8,10},{10,12},{12,14},{14,16},{16,18},{18... | collective-permute-start | bytes 270344 | tf_op jit(solution)/shard_map/ppermute | solution.py:426
  15.1 1.3 collective-permute-start.2
  16.6 3.7 %collective-permute-done.2.refs_4_ = f32[176,128]{1,0:T(8,128)S(1)} collective-permute-done((f32[176,128]{1,0:T(8,128)S(1)}, f32[176,128]{1,0:T(8,128)S(1)}, u32[]{:S(2)}, u32[]{:S(2)}) %collective-permute-start.2) | collective-permute-done | bytes 90144 | tf_op jit(solution)/shard_map/ppermute | solution.py:425
  20.4 3.1 %shard_map.103 = (f32[680,128]{1,0:T(8,128)S(1)}, f32[176,128]{1,0:T(8,128)S(1)}, f32[680,128]{1,0:T(8,128)S(1)}, f32[176,128]{1,0:T(8,128)S(1)}, f32[176,128]{1,0:T(8,128)S(1)}) custom-call(f32[8,128]{1,0:T(8,128)S(1)} %get-tuple-element.28.scalars.refs_0_, f32[680,128]{1,0:T(8,128)S(1)} %get-tuple-element.34.refs_1_, ...), custom_call_target="tpu_custom_call" | custom-call | tf_op jit(solution)/shard_map/pallas_call | solution.py:339
  23.4 4.5 %collective-permute-start.3 = (f32[176,128]{1,0:T(8,128)S(1)}, f32[176,128]{1,0:T(8,128)S(1)}, u32[]{:S(2)}, u32[]{:S(2)}) collective-permute-start(f32[176,128]{1,0:T(8,128)S(1)} %get-tuple-element.41.refs_2_), channel_id=1, source_target_pairs={{0,2},{2,4},{4,6},{6,8},{8,10},{10,12},{12,14},{14,16},{16,18},{18... | collective-permute-start | bytes 270344 | tf_op jit(solution)/shard_map/ppermute | solution.py:426
  27.9 1.3 collective-permute-start.4
  29.5 3.7 %collective-permute-done.4.refs_4_ = f32[176,128]{1,0:T(8,128)S(1)} collective-permute-done((f32[176,128]{1,0:T(8,128)S(1)}, f32[176,128]{1,0:T(8,128)S(1)}, u32[]{:S(2)}, u32[]{:S(2)}) %collective-permute-start.4) | collective-permute-done | bytes 90144 | tf_op jit(solution)/shard_map/ppermute | solution.py:425
  33.2 3.1 %shard_map.104 = (f32[680,128]{1,0:T(8,128)S(1)}, f32[176,128]{1,0:T(8,128)S(1)}, f32[680,128]{1,0:T(8,128)S(1)}, f32[176,128]{1,0:T(8,128)S(1)}, f32[176,128]{1,0:T(8,128)S(1)}) custom-call(f32[8,128]{1,0:T(8,128)S(1)} %get-tuple-element.28.scalars.refs_0_, f32[680,128]{1,0:T(8,128)S(1)} %get-tuple-element.40.refs_1_, ...), custom_call_target="tpu_custom_call" | custom-call | tf_op jit(solution)/shard_map/pallas_call | solution.py:339
  36.3 4.5 %collective-permute-start.5 = (f32[176,128]{1,0:T(8,128)S(1)}, f32[176,128]{1,0:T(8,128)S(1)}, u32[]{:S(2)}, u32[]{:S(2)}) collective-permute-start(f32[176,128]{1,0:T(8,128)S(1)} %get-tuple-element.46.refs_2_), channel_id=1, source_target_pairs={{0,2},{2,4},{4,6},{6,8},{8,10},{10,12},{12,14},{14,16},{16,18},{18... | collective-permute-start | bytes 270344 | tf_op jit(solution)/shard_map/ppermute | solution.py:426
  40.9 1.3 collective-permute-start.6
  42.7 4.1 %collective-permute-done.6.refs_4_ = f32[176,128]{1,0:T(8,128)S(1)} collective-permute-done((f32[176,128]{1,0:T(8,128)S(1)}, f32[176,128]{1,0:T(8,128)S(1)}, u32[]{:S(2)}, u32[]{:S(2)}) %collective-permute-start.6) | collective-permute-done | bytes 90144 | tf_op jit(solution)/shard_map/ppermute | solution.py:425
  47.1 13.4 %all-gather = f32[1728,128]{1,0:T(8,128)S(1)} all-gather(f32[864,128]{1,0:T(8,128)S(1)} %shard_map.105), channel_id=2, replica_groups=mesh['x'=8,'zh'=4,'zl'=2,'y'=8,'orb'=2] {'orb'}, dimensions={0}, use_global_device_ids=true | all-gather | bytes 1327104 | tf_op jit(solution)/shard_map/all_gather | solution.py:443
  62.4 11.0 %all_to_all.15 = f32[16,16,128]{2,1,0:T(8,128)} all-to-all(f32[16,16,128]{2,1,0:T(8,128)S(1)} %bitcast.19), channel_id=1, replica_groups=mesh['x'=8,'zh'=4,'zl'=2,'y'=8,'orb'=2] {'zl','y'}, dimensions={0} | all-to-all | bytes 262144 | tf_op jit(solution)/shard_map/all_to_all | solution.py:452
  74.4 42.5 %all_to_all.16 = f32[32,16,128]{2,1,0:T(8,128)} all-to-all(f32[32,16,128]{2,1,0:T(8,128)S(1)} %broadcast_in_dim.4), channel_id=1, replica_groups=mesh['x'=8,'zh'=4,'zl'=2,'y'=8,'orb'=2] {'x','zh'}, dimensions={0} | all-to-all | bytes 524288 | tf_op jit(solution)/shard_map/all_to_all | solution.py:351
  116.9 1.0 reduce_sum.19
  117.9 11.1 %all_to_all.17 = f32[16,16,128]{2,1,0:T(8,128)S(1)} all-to-all(f32[16,16,128]{2,1,0:T(8,128)S(1)} %broadcast_in_dim.5), channel_id=1, replica_groups=mesh['x'=8,'zh'=4,'zl'=2,'y'=8,'orb'=2] {'zl','y'}, dimensions={0} | all-to-all | bytes 262144 | tf_op jit(solution)/shard_map/all_to_all | solution.py:351
  129.0 6.5 %all_gather.11.gram = f32[2,256,128]{2,1,0:T(8,128)S(1)} all-gather(f32[1,256,128]{2,1,0:T(8,128)S(1)} %bitcast.18), channel_id=1, replica_groups=mesh['x'=8,'zh'=4,'zl'=2,'y'=8,'orb'=2] {'orb'}, dimensions={0}, use_global_device_ids=true | all-gather | bytes 393216 | tf_op jit(solution)/shard_map/all_gather | solution.py:454
  135.5 20.8 %shard_map.106 = f32[216,9]{1,0:T(8,128)S(1)} custom-call(f32[2,256,128]{2,1,0:T(8,128)S(1)} %all_gather.11.gram, f32[2,864,128]{2,1,0:T(8,128)S(1)} %bitcast.16, bf16[1152,1024]{1,0:T(8,128)(2,1)S(1)} %get-tuple-element.31.pick.refs_10_.refs_12_, f32[216,128]{1,0:T(8,128)S(1)} %get-tuple-element.50.interp), custom_call_target="tpu_custom_call" | custom-call | tf_op jit(solution)/shard_map/pallas_call | solution.py:339
  (16 shorter events, 4.8 us)
Async XLA Ops:
  2.8 6.1 %collective-permute-start = (f32[176,128]{1,0:T(8,128)S(1)}, f32[176,128]{1,0:T(8,128)S(1)}, u32[]{:S(2)}, u32[]{:S(2)}) collective-permute-start(f32[176,128]{1,0:T(8,128)S(1)} %get-tuple-element.30), channel_id=1, source_target_pairs={{2,0},{4,2},{6,4},{8,6},{10,8},{12,10},{14,12},{16,14},{18,16},{20... | collective-permute-start | bytes 270344 | tf_op jit(solution)/shard_map/ppermute | solution.py:379
  11.7 4.9 %collective-permute-start.1 = (f32[176,128]{1,0:T(8,128)S(1)}, f32[176,128]{1,0:T(8,128)S(1)}, u32[]{:S(2)}, u32[]{:S(2)}) collective-permute-start(f32[176,128]{1,0:T(8,128)S(1)} %get-tuple-element.35.refs_2_), channel_id=1, source_target_pairs={{0,2},{2,4},{4,6},{6,8},{8,10},{10,12},{12,14},{14,16},{16,18},{18... | collective-permute-start | bytes 270344 | tf_op jit(solution)/shard_map/ppermute | solution.py:426
  15.1 5.3 %collective-permute-start.2 = (f32[176,128]{1,0:T(8,128)S(1)}, f32[176,128]{1,0:T(8,128)S(1)}, u32[]{:S(2)}, u32[]{:S(2)}) collective-permute-start(f32[176,128]{1,0:T(8,128)S(1)} %get-tuple-element.36), channel_id=1, source_target_pairs={{2,0},{4,2},{6,4},{8,6},{10,8},{12,10},{14,12},{16,14},{18,16},{20... | collective-permute-start | bytes 270344 | tf_op jit(solution)/shard_map/ppermute | solution.py:425
  23.4 6.0 %collective-permute-start.3 = (f32[176,128]{1,0:T(8,128)S(1)}, f32[176,128]{1,0:T(8,128)S(1)}, u32[]{:S(2)}, u32[]{:S(2)}) collective-permute-start(f32[176,128]{1,0:T(8,128)S(1)} %get-tuple-element.41.refs_2_), channel_id=1, source_target_pairs={{0,2},{2,4},{4,6},{6,8},{8,10},{10,12},{12,14},{14,16},{16,18},{18... | collective-permute-start | bytes 270344 | tf_op jit(solution)/shard_map/ppermute | solution.py:426
  27.9 5.3 %collective-permute-start.4 = (f32[176,128]{1,0:T(8,128)S(1)}, f32[176,128]{1,0:T(8,128)S(1)}, u32[]{:S(2)}, u32[]{:S(2)}) collective-permute-start(f32[176,128]{1,0:T(8,128)S(1)} %get-tuple-element.42), channel_id=1, source_target_pairs={{2,0},{4,2},{6,4},{8,6},{10,8},{12,10},{14,12},{16,14},{18,16},{20... | collective-permute-start | bytes 270344 | tf_op jit(solution)/shard_map/ppermute | solution.py:425
  33.2 8.9 %copy-start.1 = (f32[676]{0:T(1024)S(1)}, f32[676]{0:T(1024)}, u32[]{:S(2)}) copy-start(f32[676]{0:T(1024)} %param.15) | copy-start | bytes 8116
  33.2 13.6 %copy-start = (f32[128]{0:T(128)S(1)}, f32[128]{0:T(128)}, u32[]{:S(2)}) copy-start(f32[128]{0:T(128)} %param.18) | copy-start | bytes 1540
  36.3 6.4 %collective-permute-start.5 = (f32[176,128]{1,0:T(8,128)S(1)}, f32[176,128]{1,0:T(8,128)S(1)}, u32[]{:S(2)}, u32[]{:S(2)}) collective-permute-start(f32[176,128]{1,0:T(8,128)S(1)} %get-tuple-element.46.refs_2_), channel_id=1, source_target_pairs={{0,2},{2,4},{4,6},{6,8},{8,10},{10,12},{12,14},{14,16},{16,18},{18... | collective-permute-start | bytes 270344 | tf_op jit(solution)/shard_map/ppermute | solution.py:426
  40.9 5.9 %collective-permute-start.6 = (f32[176,128]{1,0:T(8,128)S(1)}, f32[176,128]{1,0:T(8,128)S(1)}, u32[]{:S(2)}, u32[]{:S(2)}) collective-permute-start(f32[176,128]{1,0:T(8,128)S(1)} %get-tuple-element.47), channel_id=1, source_target_pairs={{2,0},{4,2},{6,4},{8,6},{10,8},{12,10},{14,12},{16,14},{18,16},{20... | collective-permute-start | bytes 270344 | tf_op jit(solution)/shard_map/ppermute | solution.py:425

commit v5 on v4

--- a/solution.py
+++ b/solution.py
@@ -117,7 +117,7 @@
     node = lax.broadcasted_iota(jnp.int32, (GHOST_AT, 2 * HALF), 0).astype(F32)
     spread[...] = one_hot(node, listed[0:1])
     terms[...] = jnp.zeros(terms.shape, F32)
-    terms[0:1, 0:OWN] = mass[...]
+    terms[0:1, 0:OWN] = mass[...].reshape(1, OWN)
     rest = terms[0:1]
     for term in range(3):
         part = rest.astype(BF16).astype(F32)
@@ -177,7 +177,7 @@
         product = joined(dot(left_high, both)) + dot(left_low, high)
         matrix[rows] = product + scales[cell] * square[...]
     masses[...] = jnp.ones(masses.shape, F32)
-    masses[0:1, 0:OWN] = mass[...]
+    masses[0:1, 0:OWN] = mass[...].reshape(1, OWN)
     halfwidth, centre = halfwidth_of(spectrum)
     scalars[...] = jnp.zeros(scalars.shape, F32)
     scalars[0:1] = halfwidth
@@ -319,14 +319,14 @@
     for cell in range(CELLS):
         quad[cell] = dot3(interp[...], values[cell * 128 : cell * 128 + 128])
     lax.fori_loop(0, 2, body, 0)
-    occ = jnp.concatenate([field[0, OCC_AT : OCC_AT + 1], field[1, OCC_AT : OCC_AT + 1]], axis=1)
-    weights = occ * (1.0 / ORBS)
+    occ = [column(field[half, OCC_AT : OCC_AT + 1]) for half in range(2)]
+    weights = jnp.concatenate(occ, axis=0)[:, 0:1] * (1.0 / ORBS)
     inv_high, inv_low = split(inverse[...])
     for cell in range(CELLS):
         high, low = split(quad[cell])
         dims = ((1,), (1,))
-        value = dot(high, inv_high, dims) + (dot(high, inv_low, dims) + dot(low, inv_high, dims))
-        out[:, cell : cell + 1] = jnp.sum(value * value * weights, axis=1, keepdims=True)
+        value = dot(inv_high, high, dims) + (dot(inv_low, high, dims) + dot(inv_high, low, dims))
+        out[cell : cell + 1] = jnp.sum(value * value * weights, axis=0, keepdims=True)
 
 
 def call(kernel, shapes, scratch, operands, far=0):
@@ -359,7 +359,7 @@
     down = [(i + 1, i) for i in range(count - 1)]
     up = [(i, i + 1) for i in range(count - 1)]
     listed = bottom.reshape(1, FACE)
-    mass_row = mass.reshape(1, OWN)
+    mass_row = mass
     face, own, spread = call(
         face_kernel,
         [(FACE_PAD, HALF), (OWN_PAD, HALF), (GHOST_AT, 2 * HALF, BF16)],
@@ -370,7 +370,7 @@
             pltpu.VMEM((GHOST_AT, 2 * HALF), BF16),
             pltpu.VMEM((OWN, HALF), F32),
             pltpu.VMEM((1, FACE), jnp.int32),
-            pltpu.VMEM((1, OWN), F32),
+            pltpu.VMEM((OWN,), F32),
             pltpu.SemaphoreType.DMA((3,)),
         ],
         (block.T, listed, mass_row),
@@ -403,7 +403,7 @@
             pltpu.VMEM((GAUSS, NPC), F32),
             pltpu.VMEM((CELLS, GAUSS), F32),
             pltpu.VMEM((NPC, NPC), F32),
-            pltpu.VMEM((1, OWN), F32),
+            pltpu.VMEM((OWN,), F32),
             pltpu.SemaphoreType.DMA((8,)),
         ],
         (spectrum, cell_scale, conn.T, listed, interp, potential.T, stiffness, mass_row),
@@ -446,16 +446,18 @@
     term = jnp.concatenate(
         [dot6(whole[half, :OWN_PAD], weighted, ((0,), (0,))) for half in range(2)], axis=0
     )
-    near, far = ("zl", "y"), ("x", "zh")
+    near = ("zl", "y")
     size = lax.axis_size(near)
     term = term * (1.0 / (count * OWN))
     pieces = lax.all_to_all(term.reshape(size, ORBS // size, HALF), near, 0, 0)
-    piece = jnp.sum(gather_all(jnp.sum(pieces, axis=0), far), axis=0)
+    piece = jnp.sum(pieces, axis=0)
+    for far in ("zh", "x"):
+        piece = jnp.sum(gather_all(piece, far), axis=0)
     gram = lax.all_gather(gather_all(piece, near).reshape(ORBS, HALF), "orb", axis=0)
 
     (density,) = call(
         density_kernel,
-        [(GAUSS, CELLS)],
+        [(CELLS, GAUSS)],
         [
             pltpu.VMEM((ORBS, ORBS), F32),
             pltpu.VMEM((HALF, HALF), F32),
@@ -464,7 +466,7 @@
         ],
         (gram, whole, tables[0], wide),
     )
-    return density
+    return density.T
 
 
 def solution(mesh):

time: 158 us -> 158 us (level)
  blocking collectives: 84.6 us -> 88.5 us
  local copies, waits for them, and re-layouts: 2 us -> 0.04 us
  other arithmetic: 1.93 us -> 0.05 us
    all_to_all x2 -> x3, blocking collectives: 53.7 us -> 57 us  [gather_all(): lax.all_to_all(jnp.broadcast_to(value[None], (count,) + value.shape), axe...]
    reduce_sum x2 -> x3, other arithmetic: 1.91 us -> 0.04 us  [the longest x1 0.02 us: per_device(): piece = jnp.sum(pieces, axis=0)]
where the time goes in v5:
time: 158 us; the launch traced here: 157 us
  blocking collectives  88.5 us (56%)
  Pallas kernels  35 us (22%)
  starting transfers between devices  17.6 us (11%)
  waiting for transfers between devices  14.3 us (9%)
  matrix products  1.82 us (1%)
    all_to_all x3, blocking collectives, gather_all(): lax.all_to_all(jnp.broadcast_to(value[None], (count,) + value.shape), axe...  57 us
    pallas_call x7, Pallas kernels, call(): pl.pallas_call(kernel, out_shape=out, in_specs=specs, out_specs=[in_vmem]...  35 us
    all_gather x1, blocking collectives, per_device(): whole = lax.all_gather(field, 'orb', axis=0)  13.5 us
    ppermute x3, starting transfers between devices, per_device(): from_below = lax.ppermute(ghost_sum, dom, up)  12.4 us
    ppermute x3, waiting for transfers between devices, per_device(): from_above = lax.ppermute(bottom_sum, dom, down)  11.6 us
    all_to_all x1, blocking collectives, per_device(): pieces = lax.all_to_all(term.reshape(size, ORBS // size, HALF), near, 0, 0)  10.9 us
    all_gather x1, blocking collectives, per_device(): lax.all_gather(gather_all(piece, near).reshape(ORBS, HALF), 'orb', axis=0)  7.11 us
    ppermute x3, starting transfers between devices, per_device(): from_above = lax.ppermute(bottom_sum, dom, down)  3.88 us
  transfers between devices with their start and end apart: 7, of which 7 were waited for; matrix products, arithmetic and copies ran while one was open for 0% of the time, Pallas kernels for 2%

profile of v5, /device:TPU:1, one launch (start us, length us, event | category | flops | bytes accessed | tf_op | source)
XLA Modules:
  0.0 157.4 jit_solution(2826862757250297759)
XLA Ops:
  0.0 1.5 shard_map.101
  1.5 1.3 collective-permute-start
  2.8 3.0 %shard_map.100 = (bf16[1152,1024]{1,0:T(8,128)(2,1)S(1)}, bf16[1040,1152]{1,0:T(8,128)(2,1)S(1)}, f32[1152,128]{1,0:T(8,128)S(1)}, f32[680,128]{1,0:T(8,128)S(1)...) custom-call(f32[2]{0:T(128)} %refs_0_.1, f32[9]{0:T(128)} %refs_1_.1, s32[9,125]{1,0:T(8,128)} %bitcast.23, ...), custom_call_target="tpu_custom_call" | custom-call | tf_op jit(solution)/shard_map/pallas_call | solution.py:339
  5.8 1.8 %collective-permute-done.ghost.refs_9_.refs_11_ = f32[176,128]{1,0:T(8,128)S(1)} collective-permute-done((f32[176,128]{1,0:T(8,128)S(1)}, f32[176,128]{1,0:T(8,128)S(1)}, u32[]{:S(2)}, u32[]{:S(2)}) %collective-permute-start) | collective-permute-done | bytes 90144 | tf_op jit(solution)/shard_map/ppermute | solution.py:379
  7.5 2.9 %shard_map.102 = (f32[680,128]{1,0:T(8,128)S(1)}, f32[176,128]{1,0:T(8,128)S(1)}, f32[176,128]{1,0:T(8,128)S(1)}, f32[176,128]{1,0:T(8,128)S(1)}) custom-call(f32[8,128]{1,0:T(8,128)S(1)} %get-tuple-element.28.scalars.refs_0_, f32[680,128]{1,0:T(8,128)S(1)} %get-tuple-element.29.own.refs_8_.refs_10_, ...), custom_call_target="tpu_custom_call" | custom-call | tf_op jit(solution)/shard_map/pallas_call | solution.py:339
  10.4 3.4 %collective-permute-start.1 = (f32[176,128]{1,0:T(8,128)S(1)}, f32[176,128]{1,0:T(8,128)S(1)}, u32[]{:S(2)}, u32[]{:S(2)}) collective-permute-start(f32[176,128]{1,0:T(8,128)S(1)} %get-tuple-element.35.refs_2_), channel_id=1, source_target_pairs={{0,2},{2,4},{4,6},{6,8},{8,10},{10,12},{12,14},{14,16},{16,18},{18... | collective-permute-start | bytes 270344 | tf_op jit(solution)/shard_map/ppermute | solution.py:426
  13.8 1.3 collective-permute-start.2
  15.4 3.7 %collective-permute-done.2.refs_4_ = f32[176,128]{1,0:T(8,128)S(1)} collective-permute-done((f32[176,128]{1,0:T(8,128)S(1)}, f32[176,128]{1,0:T(8,128)S(1)}, u32[]{:S(2)}, u32[]{:S(2)}) %collective-permute-start.2) | collective-permute-done | bytes 90144 | tf_op jit(solution)/shard_map/ppermute | solution.py:425
  19.1 3.1 %shard_map.103 = (f32[680,128]{1,0:T(8,128)S(1)}, f32[176,128]{1,0:T(8,128)S(1)}, f32[680,128]{1,0:T(8,128)S(1)}, f32[176,128]{1,0:T(8,128)S(1)}, f32[176,128]{1,0:T(8,128)S(1)}) custom-call(f32[8,128]{1,0:T(8,128)S(1)} %get-tuple-element.28.scalars.refs_0_, f32[680,128]{1,0:T(8,128)S(1)} %get-tuple-element.34.refs_1_, ...), custom_call_target="tpu_custom_call" | custom-call | tf_op jit(solution)/shard_map/pallas_call | solution.py:339
  22.2 4.5 %collective-permute-start.3 = (f32[176,128]{1,0:T(8,128)S(1)}, f32[176,128]{1,0:T(8,128)S(1)}, u32[]{:S(2)}, u32[]{:S(2)}) collective-permute-start(f32[176,128]{1,0:T(8,128)S(1)} %get-tuple-element.41.refs_2_), channel_id=1, source_target_pairs={{0,2},{2,4},{4,6},{6,8},{8,10},{10,12},{12,14},{14,16},{16,18},{18... | collective-permute-start | bytes 270344 | tf_op jit(solution)/shard_map/ppermute | solution.py:426
  26.7 1.3 collective-permute-start.4
  28.2 3.7 %collective-permute-done.4.refs_4_ = f32[176,128]{1,0:T(8,128)S(1)} collective-permute-done((f32[176,128]{1,0:T(8,128)S(1)}, f32[176,128]{1,0:T(8,128)S(1)}, u32[]{:S(2)}, u32[]{:S(2)}) %collective-permute-start.4) | collective-permute-done | bytes 90144 | tf_op jit(solution)/shard_map/ppermute | solution.py:425
  31.9 3.1 %shard_map.104 = (f32[680,128]{1,0:T(8,128)S(1)}, f32[176,128]{1,0:T(8,128)S(1)}, f32[680,128]{1,0:T(8,128)S(1)}, f32[176,128]{1,0:T(8,128)S(1)}, f32[176,128]{1,0:T(8,128)S(1)}) custom-call(f32[8,128]{1,0:T(8,128)S(1)} %get-tuple-element.28.scalars.refs_0_, f32[680,128]{1,0:T(8,128)S(1)} %get-tuple-element.40.refs_1_, ...), custom_call_target="tpu_custom_call" | custom-call | tf_op jit(solution)/shard_map/pallas_call | solution.py:339
  35.0 4.5 %collective-permute-start.5 = (f32[176,128]{1,0:T(8,128)S(1)}, f32[176,128]{1,0:T(8,128)S(1)}, u32[]{:S(2)}, u32[]{:S(2)}) collective-permute-start(f32[176,128]{1,0:T(8,128)S(1)} %get-tuple-element.46.refs_2_), channel_id=1, source_target_pairs={{0,2},{2,4},{4,6},{6,8},{8,10},{10,12},{12,14},{14,16},{16,18},{18... | collective-permute-start | bytes 270344 | tf_op jit(solution)/shard_map/ppermute | solution.py:426
  39.6 1.3 collective-permute-start.6
  41.4 4.1 %collective-permute-done.6.refs_4_ = f32[176,128]{1,0:T(8,128)S(1)} collective-permute-done((f32[176,128]{1,0:T(8,128)S(1)}, f32[176,128]{1,0:T(8,128)S(1)}, u32[]{:S(2)}, u32[]{:S(2)}) %collective-permute-start.6) | collective-permute-done | bytes 90144 | tf_op jit(solution)/shard_map/ppermute | solution.py:425
  45.8 13.5 %all-gather = f32[1728,128]{1,0:T(8,128)S(1)} all-gather(f32[864,128]{1,0:T(8,128)S(1)} %shard_map.105), channel_id=2, replica_groups=mesh['x'=8,'zh'=4,'zl'=2,'y'=8,'orb'=2] {'orb'}, dimensions={0}, use_global_device_ids=true | all-gather | bytes 1327104 | tf_op jit(solution)/shard_map/all_gather | solution.py:443
  60.2 0.9 fusion
  61.1 10.9 %all_to_all.20 = f32[16,16,128]{2,1,0:T(8,128)S(1)} all-to-all(f32[16,16,128]{2,1,0:T(8,128)S(1)} %bitcast.20), channel_id=1, replica_groups=mesh['x'=8,'zh'=4,'zl'=2,'y'=8,'orb'=2] {'zl','y'}, dimensions={0} | all-to-all | bytes 262144 | tf_op jit(solution)/shard_map/all_to_all | solution.py:452
  72.1 29.5 %all_to_all.21 = f32[4,16,128]{2,1,0:T(8,128)S(1)} all-to-all(f32[4,16,128]{2,1,0:T(8,128)S(1)} %broadcast_in_dim.6), channel_id=1, replica_groups=mesh['x'=8,'zh'=4,'zl'=2,'y'=8,'orb'=2] {'zh'}, dimensions={0} | all-to-all | bytes 65536 | tf_op jit(solution)/shard_map/all_to_all | solution.py:351
  101.6 16.2 %all_to_all.22 = f32[8,16,128]{2,1,0:T(8,128)S(1)} all-to-all(f32[8,16,128]{2,1,0:T(8,128)S(1)} %broadcast_in_dim.7), channel_id=1, replica_groups=mesh['x'=8,'zh'=4,'zl'=2,'y'=8,'orb'=2] {'x'}, dimensions={0} | all-to-all | bytes 131072 | tf_op jit(solution)/shard_map/all_to_all | solution.py:351
  117.9 11.3 %all_to_all.23 = f32[16,16,128]{2,1,0:T(8,128)S(1)} all-to-all(f32[16,16,128]{2,1,0:T(8,128)S(1)} %broadcast_in_dim.8), channel_id=1, replica_groups=mesh['x'=8,'zh'=4,'zl'=2,'y'=8,'orb'=2] {'zl','y'}, dimensions={0} | all-to-all | bytes 262144 | tf_op jit(solution)/shard_map/all_to_all | solution.py:351
  129.1 7.1 %all_gather.11.gram = f32[2,256,128]{2,1,0:T(8,128)S(1)} all-gather(f32[1,256,128]{2,1,0:T(8,128)S(1)} %bitcast.19), channel_id=1, replica_groups=mesh['x'=8,'zh'=4,'zl'=2,'y'=8,'orb'=2] {'orb'}, dimensions={0}, use_global_device_ids=true | all-gather | bytes 393216 | tf_op jit(solution)/shard_map/all_gather | solution.py:456
  136.2 21.2 %shard_map.106 = f32[9,216]{1,0:T(8,128)} custom-call(f32[2,256,128]{2,1,0:T(8,128)S(1)} %all_gather.11.gram, f32[2,864,128]{2,1,0:T(8,128)S(1)} %bitcast.17, bf16[1152,1024]{1,0:T(8,128)(2,1)S(1)} %get-tuple-element.31.pick.refs_10_.refs_12_, f32[216,128]{1,0:T(8,128)S(1)} %get-tuple-element.50.interp), custom_call_target="tpu_custom_call" | custom-call | tf_op jit(solution)/shard_map/pallas_call | solution.py:339
  (17 shorter events, 2.3 us)
Async XLA Ops:
  1.5 6.1 %collective-permute-start = (f32[176,128]{1,0:T(8,128)S(1)}, f32[176,128]{1,0:T(8,128)S(1)}, u32[]{:S(2)}, u32[]{:S(2)}) collective-permute-start(f32[176,128]{1,0:T(8,128)S(1)} %get-tuple-element.30), channel_id=1, source_target_pairs={{2,0},{4,2},{6,4},{8,6},{10,8},{12,10},{14,12},{16,14},{18,16},{20... | collective-permute-start | bytes 270344 | tf_op jit(solution)/shard_map/ppermute | solution.py:379
  10.4 4.9 %collective-permute-start.1 = (f32[176,128]{1,0:T(8,128)S(1)}, f32[176,128]{1,0:T(8,128)S(1)}, u32[]{:S(2)}, u32[]{:S(2)}) collective-permute-start(f32[176,128]{1,0:T(8,128)S(1)} %get-tuple-element.35.refs_2_), channel_id=1, source_target_pairs={{0,2},{2,4},{4,6},{6,8},{8,10},{10,12},{12,14},{14,16},{16,18},{18... | collective-permute-start | bytes 270344 | tf_op jit(solution)/shard_map/ppermute | solution.py:426
  13.8 5.3 %collective-permute-start.2 = (f32[176,128]{1,0:T(8,128)S(1)}, f32[176,128]{1,0:T(8,128)S(1)}, u32[]{:S(2)}, u32[]{:S(2)}) collective-permute-start(f32[176,128]{1,0:T(8,128)S(1)} %get-tuple-element.36), channel_id=1, source_target_pairs={{2,0},{4,2},{6,4},{8,6},{10,8},{12,10},{14,12},{16,14},{18,16},{20... | collective-permute-start | bytes 270344 | tf_op jit(solution)/shard_map/ppermute | solution.py:425
  22.2 6.0 %collective-permute-start.3 = (f32[176,128]{1,0:T(8,128)S(1)}, f32[176,128]{1,0:T(8,128)S(1)}, u32[]{:S(2)}, u32[]{:S(2)}) collective-permute-start(f32[176,128]{1,0:T(8,128)S(1)} %get-tuple-element.41.refs_2_), channel_id=1, source_target_pairs={{0,2},{2,4},{4,6},{6,8},{8,10},{10,12},{12,14},{14,16},{16,18},{18... | collective-permute-start | bytes 270344 | tf_op jit(solution)/shard_map/ppermute | solution.py:426
  26.7 5.3 %collective-permute-start.4 = (f32[176,128]{1,0:T(8,128)S(1)}, f32[176,128]{1,0:T(8,128)S(1)}, u32[]{:S(2)}, u32[]{:S(2)}) collective-permute-start(f32[176,128]{1,0:T(8,128)S(1)} %get-tuple-element.42), channel_id=1, source_target_pairs={{2,0},{4,2},{6,4},{8,6},{10,8},{12,10},{14,12},{16,14},{18,16},{20... | collective-permute-start | bytes 270344 | tf_op jit(solution)/shard_map/ppermute | solution.py:425
  31.9 8.9 %copy-start.1 = (f32[676]{0:T(1024)S(1)}, f32[676]{0:T(1024)}, u32[]{:S(2)}) copy-start(f32[676]{0:T(1024)} %refs_2_.1) | copy-start | bytes 8116
  31.9 13.6 %copy-start = (f32[128]{0:T(128)S(1)}, f32[128]{0:T(128)}, u32[]{:S(2)}) copy-start(f32[128]{0:T(128)} %param.18) | copy-start | bytes 1540
  35.0 6.4 %collective-permute-start.5 = (f32[176,128]{1,0:T(8,128)S(1)}, f32[176,128]{1,0:T(8,128)S(1)}, u32[]{:S(2)}, u32[]{:S(2)}) collective-permute-start(f32[176,128]{1,0:T(8,128)S(1)} %get-tuple-element.46.refs_2_), channel_id=1, source_target_pairs={{0,2},{2,4},{4,6},{6,8},{8,10},{10,12},{12,14},{14,16},{16,18},{18... | collective-permute-start | bytes 270344 | tf_op jit(solution)/shard_map/ppermute | solution.py:426
  39.6 5.9 %collective-permute-start.6 = (f32[176,128]{1,0:T(8,128)S(1)}, f32[176,128]{1,0:T(8,128)S(1)}, u32[]{:S(2)}, u32[]{:S(2)}) collective-permute-start(f32[176,128]{1,0:T(8,128)S(1)} %get-tuple-element.47), channel_id=1, source_target_pairs={{2,0},{4,2},{6,4},{8,6},{10,8},{12,10},{14,12},{16,14},{18,16},{20... | collective-permute-start | bytes 270344 | tf_op jit(solution)/shard_map/ppermute | solution.py:425

commit v6 on v5

--- a/solution.py
+++ b/solution.py
@@ -241,7 +241,6 @@
 
 def reciprocal(value):
     guess = pl.reciprocal(value, approx=True)
-    guess = guess * (2.0 - value * guess)
     return guess * (2.0 - value * guess)
 
 

time: 158 us -> 156 us (0.987)
  no operation moved by 1% of the time
where the time goes in v6:
time: 156 us
  blocking collectives  88.5 us (57%)
  Pallas kernels  33.5 us (21%)
  starting transfers between devices  17.6 us (11%)
  waiting for transfers between devices  14.3 us (9%)
  matrix products  1.82 us (1%)
    all_to_all x3, blocking collectives, gather_all(): lax.all_to_all(jnp.broadcast_to(value[None], (count,) + value.shape), axe...  57 us
    pallas_call x7, Pallas kernels, call(): pl.pallas_call(kernel, out_shape=out, in_specs=specs, out_specs=[in_vmem]...  33.5 us
    all_gather x1, blocking collectives, per_device(): whole = lax.all_gather(field, 'orb', axis=0)  13.5 us
    ppermute x3, starting transfers between devices, per_device(): from_below = lax.ppermute(ghost_sum, dom, up)  12.4 us
    ppermute x3, waiting for transfers between devices, per_device(): from_above = lax.ppermute(bottom_sum, dom, down)  11.6 us
    all_to_all x1, blocking collectives, per_device(): pieces = lax.all_to_all(term.reshape(size, ORBS // size, HALF), near, 0, 0)  10.9 us
    all_gather x1, blocking collectives, per_device(): lax.all_gather(gather_all(piece, near).reshape(ORBS, HALF), 'orb', axis=0)  7.11 us
    ppermute x3, starting transfers between devices, per_device(): from_above = lax.ppermute(bottom_sum, dom, down)  3.88 us
  transfers between devices with their start and end apart: 7, of which 7 were waited for; matrix products, arithmetic and copies ran while one was open for 0% of the time, Pallas kernels for 2%

profile of v6, /device:TPU:1, one launch (start us, length us, event | category | flops | bytes accessed | tf_op | source)
XLA Modules:
  0.0 155.9 jit_solution(17673378223451853512)
XLA Ops:
  0.0 1.5 shard_map.101
  1.5 1.3 collective-permute-start
  2.8 3.0 %shard_map.100 = (bf16[1152,1024]{1,0:T(8,128)(2,1)S(1)}, bf16[1040,1152]{1,0:T(8,128)(2,1)S(1)}, f32[1152,128]{1,0:T(8,128)S(1)}, f32[680,128]{1,0:T(8,128)S(1)...) custom-call(f32[2]{0:T(128)} %refs_0_.1, f32[9]{0:T(128)} %refs_1_.1, s32[9,125]{1,0:T(8,128)} %bitcast.23, ...), custom_call_target="tpu_custom_call" | custom-call | tf_op jit(solution)/shard_map/pallas_call | solution.py:338
  5.8 1.8 %collective-permute-done.ghost.refs_9_.refs_11_ = f32[176,128]{1,0:T(8,128)S(1)} collective-permute-done((f32[176,128]{1,0:T(8,128)S(1)}, f32[176,128]{1,0:T(8,128)S(1)}, u32[]{:S(2)}, u32[]{:S(2)}) %collective-permute-start) | collective-permute-done | bytes 90144 | tf_op jit(solution)/shard_map/ppermute | solution.py:378
  7.5 2.9 %shard_map.102 = (f32[680,128]{1,0:T(8,128)S(1)}, f32[176,128]{1,0:T(8,128)S(1)}, f32[176,128]{1,0:T(8,128)S(1)}, f32[176,128]{1,0:T(8,128)S(1)}) custom-call(f32[8,128]{1,0:T(8,128)S(1)} %get-tuple-element.28.scalars.refs_0_, f32[680,128]{1,0:T(8,128)S(1)} %get-tuple-element.29.own.refs_8_.refs_10_, ...), custom_call_target="tpu_custom_call" | custom-call | tf_op jit(solution)/shard_map/pallas_call | solution.py:338
  10.4 3.4 %collective-permute-start.1 = (f32[176,128]{1,0:T(8,128)S(1)}, f32[176,128]{1,0:T(8,128)S(1)}, u32[]{:S(2)}, u32[]{:S(2)}) collective-permute-start(f32[176,128]{1,0:T(8,128)S(1)} %get-tuple-element.35.refs_2_), channel_id=1, source_target_pairs={{0,2},{2,4},{4,6},{6,8},{8,10},{10,12},{12,14},{14,16},{16,18},{18... | collective-permute-start | bytes 270344 | tf_op jit(solution)/shard_map/ppermute | solution.py:425
  13.8 1.3 collective-permute-start.2
  15.4 3.7 %collective-permute-done.2.refs_4_ = f32[176,128]{1,0:T(8,128)S(1)} collective-permute-done((f32[176,128]{1,0:T(8,128)S(1)}, f32[176,128]{1,0:T(8,128)S(1)}, u32[]{:S(2)}, u32[]{:S(2)}) %collective-permute-start.2) | collective-permute-done | bytes 90144 | tf_op jit(solution)/shard_map/ppermute | solution.py:424
  19.1 3.1 %shard_map.103 = (f32[680,128]{1,0:T(8,128)S(1)}, f32[176,128]{1,0:T(8,128)S(1)}, f32[680,128]{1,0:T(8,128)S(1)}, f32[176,128]{1,0:T(8,128)S(1)}, f32[176,128]{1,0:T(8,128)S(1)}) custom-call(f32[8,128]{1,0:T(8,128)S(1)} %get-tuple-element.28.scalars.refs_0_, f32[680,128]{1,0:T(8,128)S(1)} %get-tuple-element.34.refs_1_, ...), custom_call_target="tpu_custom_call" | custom-call | tf_op jit(solution)/shard_map/pallas_call | solution.py:338
  22.2 4.5 %collective-permute-start.3 = (f32[176,128]{1,0:T(8,128)S(1)}, f32[176,128]{1,0:T(8,128)S(1)}, u32[]{:S(2)}, u32[]{:S(2)}) collective-permute-start(f32[176,128]{1,0:T(8,128)S(1)} %get-tuple-element.41.refs_2_), channel_id=1, source_target_pairs={{0,2},{2,4},{4,6},{6,8},{8,10},{10,12},{12,14},{14,16},{16,18},{18... | collective-permute-start | bytes 270344 | tf_op jit(solution)/shard_map/ppermute | solution.py:425
  26.7 1.3 collective-permute-start.4
  28.2 3.7 %collective-permute-done.4.refs_4_ = f32[176,128]{1,0:T(8,128)S(1)} collective-permute-done((f32[176,128]{1,0:T(8,128)S(1)}, f32[176,128]{1,0:T(8,128)S(1)}, u32[]{:S(2)}, u32[]{:S(2)}) %collective-permute-start.4) | collective-permute-done | bytes 90144 | tf_op jit(solution)/shard_map/ppermute | solution.py:424
  31.9 3.1 %shard_map.104 = (f32[680,128]{1,0:T(8,128)S(1)}, f32[176,128]{1,0:T(8,128)S(1)}, f32[680,128]{1,0:T(8,128)S(1)}, f32[176,128]{1,0:T(8,128)S(1)}, f32[176,128]{1,0:T(8,128)S(1)}) custom-call(f32[8,128]{1,0:T(8,128)S(1)} %get-tuple-element.28.scalars.refs_0_, f32[680,128]{1,0:T(8,128)S(1)} %get-tuple-element.40.refs_1_, ...), custom_call_target="tpu_custom_call" | custom-call | tf_op jit(solution)/shard_map/pallas_call | solution.py:338
  35.0 4.5 %collective-permute-start.5 = (f32[176,128]{1,0:T(8,128)S(1)}, f32[176,128]{1,0:T(8,128)S(1)}, u32[]{:S(2)}, u32[]{:S(2)}) collective-permute-start(f32[176,128]{1,0:T(8,128)S(1)} %get-tuple-element.46.refs_2_), channel_id=1, source_target_pairs={{0,2},{2,4},{4,6},{6,8},{8,10},{10,12},{12,14},{14,16},{16,18},{18... | collective-permute-start | bytes 270344 | tf_op jit(solution)/shard_map/ppermute | solution.py:425
  39.6 1.3 collective-permute-start.6
  41.4 4.1 %collective-permute-done.6.refs_4_ = f32[176,128]{1,0:T(8,128)S(1)} collective-permute-done((f32[176,128]{1,0:T(8,128)S(1)}, f32[176,128]{1,0:T(8,128)S(1)}, u32[]{:S(2)}, u32[]{:S(2)}) %collective-permute-start.6) | collective-permute-done | bytes 90144 | tf_op jit(solution)/shard_map/ppermute | solution.py:424
  45.8 13.5 %all-gather = f32[1728,128]{1,0:T(8,128)S(1)} all-gather(f32[864,128]{1,0:T(8,128)S(1)} %shard_map.105), channel_id=2, replica_groups=mesh['x'=8,'zh'=4,'zl'=2,'y'=8,'orb'=2] {'orb'}, dimensions={0}, use_global_device_ids=true | all-gather | bytes 1327104 | tf_op jit(solution)/shard_map/all_gather | solution.py:442
  60.2 0.9 fusion
  61.1 10.9 %all_to_all.20 = f32[16,16,128]{2,1,0:T(8,128)S(1)} all-to-all(f32[16,16,128]{2,1,0:T(8,128)S(1)} %bitcast.20), channel_id=1, replica_groups=mesh['x'=8,'zh'=4,'zl'=2,'y'=8,'orb'=2] {'zl','y'}, dimensions={0} | all-to-all | bytes 262144 | tf_op jit(solution)/shard_map/all_to_all | solution.py:451
  72.1 29.5 %all_to_all.21 = f32[4,16,128]{2,1,0:T(8,128)S(1)} all-to-all(f32[4,16,128]{2,1,0:T(8,128)S(1)} %broadcast_in_dim.6), channel_id=1, replica_groups=mesh['x'=8,'zh'=4,'zl'=2,'y'=8,'orb'=2] {'zh'}, dimensions={0} | all-to-all | bytes 65536 | tf_op jit(solution)/shard_map/all_to_all | solution.py:350
  101.6 16.2 %all_to_all.22 = f32[8,16,128]{2,1,0:T(8,128)S(1)} all-to-all(f32[8,16,128]{2,1,0:T(8,128)S(1)} %broadcast_in_dim.7), channel_id=1, replica_groups=mesh['x'=8,'zh'=4,'zl'=2,'y'=8,'orb'=2] {'x'}, dimensions={0} | all-to-all | bytes 131072 | tf_op jit(solution)/shard_map/all_to_all | solution.py:350
  117.9 11.3 %all_to_all.23 = f32[16,16,128]{2,1,0:T(8,128)S(1)} all-to-all(f32[16,16,128]{2,1,0:T(8,128)S(1)} %broadcast_in_dim.8), channel_id=1, replica_groups=mesh['x'=8,'zh'=4,'zl'=2,'y'=8,'orb'=2] {'zl','y'}, dimensions={0} | all-to-all | bytes 262144 | tf_op jit(solution)/shard_map/all_to_all | solution.py:350
  129.1 7.1 %all_gather.11.gram = f32[2,256,128]{2,1,0:T(8,128)S(1)} all-gather(f32[1,256,128]{2,1,0:T(8,128)S(1)} %bitcast.19), channel_id=1, replica_groups=mesh['x'=8,'zh'=4,'zl'=2,'y'=8,'orb'=2] {'orb'}, dimensions={0}, use_global_device_ids=true | all-gather | bytes 393216 | tf_op jit(solution)/shard_map/all_gather | solution.py:455
  136.2 19.7 %shard_map.106 = f32[9,216]{1,0:T(8,128)} custom-call(f32[2,256,128]{2,1,0:T(8,128)S(1)} %all_gather.11.gram, f32[2,864,128]{2,1,0:T(8,128)S(1)} %bitcast.17, bf16[1152,1024]{1,0:T(8,128)(2,1)S(1)} %get-tuple-element.31.pick.refs_10_.refs_12_, f32[216,128]{1,0:T(8,128)S(1)} %get-tuple-element.50.interp), custom_call_target="tpu_custom_call" | custom-call | tf_op jit(solution)/shard_map/pallas_call | solution.py:338
  (17 shorter events, 2.3 us)
Async XLA Ops:
  1.5 6.1 %collective-permute-start = (f32[176,128]{1,0:T(8,128)S(1)}, f32[176,128]{1,0:T(8,128)S(1)}, u32[]{:S(2)}, u32[]{:S(2)}) collective-permute-start(f32[176,128]{1,0:T(8,128)S(1)} %get-tuple-element.30), channel_id=1, source_target_pairs={{2,0},{4,2},{6,4},{8,6},{10,8},{12,10},{14,12},{16,14},{18,16},{20... | collective-permute-start | bytes 270344 | tf_op jit(solution)/shard_map/ppermute | solution.py:378
  10.4 4.9 %collective-permute-start.1 = (f32[176,128]{1,0:T(8,128)S(1)}, f32[176,128]{1,0:T(8,128)S(1)}, u32[]{:S(2)}, u32[]{:S(2)}) collective-permute-start(f32[176,128]{1,0:T(8,128)S(1)} %get-tuple-element.35.refs_2_), channel_id=1, source_target_pairs={{0,2},{2,4},{4,6},{6,8},{8,10},{10,12},{12,14},{14,16},{16,18},{18... | collective-permute-start | bytes 270344 | tf_op jit(solution)/shard_map/ppermute | solution.py:425
  13.8 5.3 %collective-permute-start.2 = (f32[176,128]{1,0:T(8,128)S(1)}, f32[176,128]{1,0:T(8,128)S(1)}, u32[]{:S(2)}, u32[]{:S(2)}) collective-permute-start(f32[176,128]{1,0:T(8,128)S(1)} %get-tuple-element.36), channel_id=1, source_target_pairs={{2,0},{4,2},{6,4},{8,6},{10,8},{12,10},{14,12},{16,14},{18,16},{20... | collective-permute-start | bytes 270344 | tf_op jit(solution)/shard_map/ppermute | solution.py:424
  22.2 6.0 %collective-permute-start.3 = (f32[176,128]{1,0:T(8,128)S(1)}, f32[176,128]{1,0:T(8,128)S(1)}, u32[]{:S(2)}, u32[]{:S(2)}) collective-permute-start(f32[176,128]{1,0:T(8,128)S(1)} %get-tuple-element.41.refs_2_), channel_id=1, source_target_pairs={{0,2},{2,4},{4,6},{6,8},{8,10},{10,12},{12,14},{14,16},{16,18},{18... | collective-permute-start | bytes 270344 | tf_op jit(solution)/shard_map/ppermute | solution.py:425
  26.7 5.3 %collective-permute-start.4 = (f32[176,128]{1,0:T(8,128)S(1)}, f32[176,128]{1,0:T(8,128)S(1)}, u32[]{:S(2)}, u32[]{:S(2)}) collective-permute-start(f32[176,128]{1,0:T(8,128)S(1)} %get-tuple-element.42), channel_id=1, source_target_pairs={{2,0},{4,2},{6,4},{8,6},{10,8},{12,10},{14,12},{16,14},{18,16},{20... | collective-permute-start | bytes 270344 | tf_op jit(solution)/shard_map/ppermute | solution.py:424
  31.9 8.9 %copy-start.1 = (f32[676]{0:T(1024)S(1)}, f32[676]{0:T(1024)}, u32[]{:S(2)}) copy-start(f32[676]{0:T(1024)} %refs_2_.1) | copy-start | bytes 8116
  31.9 13.6 %copy-start = (f32[128]{0:T(128)S(1)}, f32[128]{0:T(128)}, u32[]{:S(2)}) copy-start(f32[128]{0:T(128)} %param.18) | copy-start | bytes 1540
  35.0 6.4 %collective-permute-start.5 = (f32[176,128]{1,0:T(8,128)S(1)}, f32[176,128]{1,0:T(8,128)S(1)}, u32[]{:S(2)}, u32[]{:S(2)}) collective-permute-start(f32[176,128]{1,0:T(8,128)S(1)} %get-tuple-element.46.refs_2_), channel_id=1, source_target_pairs={{0,2},{2,4},{4,6},{6,8},{8,10},{10,12},{12,14},{14,16},{16,18},{18... | collective-permute-start | bytes 270344 | tf_op jit(solution)/shard_map/ppermute | solution.py:425
  39.6 5.9 %collective-permute-start.6 = (f32[176,128]{1,0:T(8,128)S(1)}, f32[176,128]{1,0:T(8,128)S(1)}, u32[]{:S(2)}, u32[]{:S(2)}) collective-permute-start(f32[176,128]{1,0:T(8,128)S(1)} %get-tuple-element.47), channel_id=1, source_target_pairs={{2,0},{4,2},{6,4},{8,6},{10,8},{12,10},{14,12},{16,14},{18,16},{20... | collective-permute-start | bytes 270344 | tf_op jit(solution)/shard_map/ppermute | solution.py:424
